TPU v7x, 512 devices: a whole 4x4x16 slice. The times are simulated.
512 devices in a mesh: row: 16 (over z_hi, y, core), col: 32 (over x, z_lo).
Axes of the slice: x: 4, y: 4, z: 16 (z_hi: 2, z_lo: 8; z = z_hi * 8 + z_lo), core: 2. Of those that a mesh axis runs over, the one named last changes fastest.
Arguments:
- left_blocks: bfloat16 [16, 32, 2, 8, 64, 64], P('row', 'col'), may hold values from -0.375 to 0.375
- left_cols: int32 [16, 32, 2, 8], P('row', 'col'), may hold values from 0 to 15, all different within a row
- right_blocks: bfloat16 [16, 32, 16, 6, 64, 64], P('row', 'col'), may hold values from -6 to 6
- right_cols: int32 [16, 32, 16, 6], P('row', 'col'), may hold values from 0 to 15, all different within a row
- out_cols: int32 [16, 32, 2, 8], P('row', 'col'), may hold values from 0 to 15, all different within a row
Outputs:
- product: float32 [16, 32, 2, 8, 64, 64], P('row', 'col')
Inputs may be any that keep to these rules, and one draw needn't show every extreme that they name: `left_cols`: the entries of one block row are distinct. `right_cols`: the entries of one block row are distinct. `out_cols`: the entries of one block row are distinct.
All inputs are finite; a program needn't handle non-finite values.
Results may differ from a plain program's by a relative error of at most 0.0003.
Values may be sent and summed in bfloat16 or wider, within the bound.
A program may use at most 64 MiB of HBM per device.

v0:
```python
import jax
import jax.numpy as jnp
from jax import lax
from jax.sharding import PartitionSpec as P

TICKS = 8


def shifted(value, axis, steps):
    count = lax.axis_size(axis)
    pairs = [(source, (source + steps) % count) for source in range(count)]
    return lax.ppermute(value, axis, pairs)


def one_tick(left, left_cols, right, right_cols, pattern):
    inner = right.shape[0]
    pick_row = (left_cols[:, :, None] == jnp.arange(inner, dtype=jnp.int32)[None, None, :]).astype(
        jnp.float32
    )
    match = (right_cols[None, None, :, :] == pattern[:, :, None, None]).astype(jnp.float32)
    select = jnp.einsum("iak,iokb->iaokb", pick_row, match).astype(jnp.bfloat16)
    chosen = jnp.einsum(
        "iaokb,kbyz->iaoyz", select, right, preferred_element_type=jnp.float32
    ).astype(jnp.bfloat16)
    return jnp.einsum("iaxy,iaoyz->ioxz", left, chosen, preferred_element_type=jnp.float32)


def on_device(left_blocks, left_cols, right_blocks, right_cols, out_cols):
    left = left_blocks[0, 0]
    left_index = left_cols[0, 0]
    right = right_blocks[0, 0]
    right_index = right_cols[0, 0]
    pattern = out_cols[0, 0]
    total = jnp.zeros((left.shape[0], pattern.shape[1], left.shape[2], left.shape[3]), jnp.float32)
    left, left_index, right, right_index = shifted(
        (left, left_index, right, right_index), "col", TICKS - 1
    )
    for step in range(TICKS):
        total = total + one_tick(left, left_index, right, right_index, pattern)
        if step + 1 < TICKS:
            left, left_index, right, right_index = shifted(
                (left, left_index, right, right_index), "col", -1
            )
            left, left_index = shifted((left, left_index), "row", 1)
    return total[None, None]


def solution(mesh):
    in_specs = (
        P("row", "col", None, None, None, None),
        P("row", "col", None, None),
        P("row", "col", None, None, None, None),
        P("row", "col", None, None),
        P("row", "col", None, None),
    )
    out_specs = P("row", "col", None, None, None, None)
    return jax.shard_map(
        on_device, mesh=mesh, in_specs=in_specs, out_specs=out_specs, check_vma=False
    )
```

profile of v0, /device:TPU:24, one launch (start us, length us, event | category | flops | bytes accessed | tf_op | source)
XLA Modules:
  0.0 706.2 jit_solution(17924191292688245077)
XLA Ops:
  0.0 13.1 %collective-permute-start.1 = (s32[2,8]{1,0:T(2,128)}, s32[2,8]{1,0:T(2,128)S(1)}, u32[]{:S(2)}, u32[]{:S(2)}) collective-permute-start(s32[2,8]{1,0:T(2,128)} %bitcast.231), channel_id=1, source_target_pairs={{0,7},{1,8},{2,9},{3,10},{4,11},{5,12},{6,13},{7,14},{8,15},{9,16}... | collective-permute-start | bytes 200 | tf_op jit(solution)/shard_map/ppermute | solution.py:12
  14.6 13.0 %collective-permute-start.5 = (s32[2,8]{1,0:T(2,128)S(1)}, s32[2,8]{1,0:T(2,128)S(1)}, u32[]{:S(2)}, u32[]{:S(2)}) collective-permute-start(s32[2,8]{1,0:T(2,128)S(1)} %collective-permute-done.1), channel_id=1, source_target_pairs={{0,31},{1,0},{2,1},{3,2},{4,3},{5,4},{6,5},{7,6},{8,7},{9,8},{10,9... | collective-permute-start | bytes 200 | tf_op jit(solution)/shard_map/ppermute | solution.py:12
  31.5 8.8 %collective-permute-start.2 = (bf16[16,6,64,64]{3,2,1,0:T(8,128)(2,1)}, bf16[16,6,64,64]{3,2,1,0:T(8,128)(2,1)}, u32[]{:S(2)}, u32[]{:S(2)}) collective-permute-start(bf16[16,6,64,64]{3,2,1,0:T(8,128)(2,1)} %bitcast.229), channel_id=1, source_target_pairs={{0,7},{1,8},{2,9},{3,10},{4,11},{5,12},{6,13},{7,14},{8,15},{9,16}... | collective-permute-start | bytes 2359304 | tf_op jit(solution)/shard_map/ppermute | solution.py:12
  40.3 6.3 collective-permute-start.11
  46.7 1.9 collective-permute-start.3
  48.6 21.6 %collective-permute-done.11 = s32[2,8]{1,0:T(2,128)S(1)} collective-permute-done((s32[2,8]{1,0:T(2,128)S(1)}, s32[2,8]{1,0:T(2,128)S(1)}, u32[]{:S(2)}, u32[]{:S(2)}) %collective-permute-start.11) | collective-permute-done | bytes 96 | tf_op jit(solution)/shard_map/ppermute | solution.py:12
  70.2 10.0 %collective-permute-start.12 = (s32[2,8]{1,0:T(2,128)S(1)}, s32[2,8]{1,0:T(2,128)S(1)}, u32[]{:S(2)}, u32[]{:S(2)}) collective-permute-start(s32[2,8]{1,0:T(2,128)S(1)} %collective-permute-done.11), channel_id=1, source_target_pairs={{0,32},{32,64},{64,96},{96,128},{128,160},{160,192},{192,224},{224... | collective-permute-start | bytes 200 | tf_op jit(solution)/shard_map/ppermute | solution.py:12
  81.0 12.7 %collective-permute-start.17 = (s32[2,8]{1,0:T(2,128)S(1)}, s32[2,8]{1,0:T(2,128)S(1)}, u32[]{:S(2)}, u32[]{:S(2)}) collective-permute-start(s32[2,8]{1,0:T(2,128)S(1)} %collective-permute-done.12), channel_id=1, source_target_pairs={{0,31},{1,0},{2,1},{3,2},{4,3},{5,4},{6,5},{7,6},{8,7},{9,8},{10,9... | collective-permute-start | bytes 200 | tf_op jit(solution)/shard_map/ppermute | solution.py:12
  95.7 4.3 collective-permute-start.18
  100.8 12.0 %collective-permute-start.23 = (s32[2,8]{1,0:T(2,128)S(1)}, s32[2,8]{1,0:T(2,128)S(1)}, u32[]{:S(2)}, u32[]{:S(2)}) collective-permute-start(s32[2,8]{1,0:T(2,128)S(1)} %collective-permute-done.18), channel_id=1, source_target_pairs={{0,31},{1,0},{2,1},{3,2},{4,3},{5,4},{6,5},{7,6},{8,7},{9,8},{10,9... | collective-permute-start | bytes 200 | tf_op jit(solution)/shard_map/ppermute | solution.py:12
  114.8 15.1 %collective-permute-start.24 = (s32[2,8]{1,0:T(2,128)S(1)}, s32[2,8]{1,0:T(2,128)S(1)}, u32[]{:S(2)}, u32[]{:S(2)}) collective-permute-start(s32[2,8]{1,0:T(2,128)S(1)} %collective-permute-done.23), channel_id=1, source_target_pairs={{0,32},{32,64},{64,96},{96,128},{128,160},{160,192},{192,224},{224... | collective-permute-start | bytes 200 | tf_op jit(solution)/shard_map/ppermute | solution.py:12
  130.7 11.3 %collective-permute-start.29 = (s32[2,8]{1,0:T(2,128)S(1)}, s32[2,8]{1,0:T(2,128)S(1)}, u32[]{:S(2)}, u32[]{:S(2)}) collective-permute-start(s32[2,8]{1,0:T(2,128)S(1)} %collective-permute-done.24), channel_id=1, source_target_pairs={{0,31},{1,0},{2,1},{3,2},{4,3},{5,4},{6,5},{7,6},{8,7},{9,8},{10,9... | collective-permute-start | bytes 200 | tf_op jit(solution)/shard_map/ppermute | solution.py:12
  144.0 15.8 %collective-permute-start.30 = (s32[2,8]{1,0:T(2,128)S(1)}, s32[2,8]{1,0:T(2,128)S(1)}, u32[]{:S(2)}, u32[]{:S(2)}) collective-permute-start(s32[2,8]{1,0:T(2,128)S(1)} %collective-permute-done.29), channel_id=1, source_target_pairs={{0,32},{32,64},{64,96},{96,128},{128,160},{160,192},{192,224},{224... | collective-permute-start | bytes 200 | tf_op jit(solution)/shard_map/ppermute | solution.py:12
  159.8 11.3 %collective-permute-start.22 = (s32[16,6]{0,1:T(8,128)S(1)}, s32[16,6]{0,1:T(8,128)S(1)}, u32[]{:S(2)}, u32[]{:S(2)}) collective-permute-start(s32[16,6]{0,1:T(8,128)S(1)} %collective-permute-done.16), channel_id=1, source_target_pairs={{0,31},{1,0},{2,1},{3,2},{4,3},{5,4},{6,5},{7,6},{8,7},{9,8},{10,9... | collective-permute-start | bytes 1160 | tf_op jit(solution)/shard_map/ppermute | solution.py:12
  173.1 12.2 %collective-permute-start.28 = (s32[16,6]{0,1:T(8,128)S(1)}, s32[16,6]{0,1:T(8,128)S(1)}, u32[]{:S(2)}, u32[]{:S(2)}) collective-permute-start(s32[16,6]{0,1:T(8,128)S(1)} %collective-permute-done.22), channel_id=1, source_target_pairs={{0,31},{1,0},{2,1},{3,2},{4,3},{5,4},{6,5},{7,6},{8,7},{9,8},{10,9... | collective-permute-start | bytes 1160 | tf_op jit(solution)/shard_map/ppermute | solution.py:12
  185.3 14.7 %collective-permute-start.36 = (s32[2,8]{1,0:T(2,128)S(1)}, s32[2,8]{1,0:T(2,128)S(1)}, u32[]{:S(2)}, u32[]{:S(2)}) collective-permute-start(s32[2,8]{1,0:T(2,128)S(1)} %collective-permute-done.35), channel_id=1, source_target_pairs={{0,32},{32,64},{64,96},{96,128},{128,160},{160,192},{192,224},{224... | collective-permute-start | bytes 200 | tf_op jit(solution)/shard_map/ppermute | solution.py:12
  200.9 2.2 collective-permute-start.41
  206.3 13.2 %collective-permute-start.42 = (s32[2,8]{1,0:T(2,128)S(1)}, s32[2,8]{1,0:T(2,128)S(1)}, u32[]{:S(2)}, u32[]{:S(2)}) collective-permute-start(s32[2,8]{1,0:T(2,128)S(1)} %collective-permute-done.41), channel_id=1, source_target_pairs={{0,32},{32,64},{64,96},{96,128},{128,160},{160,192},{192,224},{224... | collective-permute-start | bytes 200 | tf_op jit(solution)/shard_map/ppermute | solution.py:12
  219.5 11.3 %collective-permute-start.40 = (s32[16,6]{0,1:T(8,128)S(1)}, s32[16,6]{0,1:T(8,128)S(1)}, u32[]{:S(2)}, u32[]{:S(2)}) collective-permute-start(s32[16,6]{0,1:T(8,128)S(1)} %collective-permute-done.34), channel_id=1, source_target_pairs={{0,31},{1,0},{2,1},{3,2},{4,3},{5,4},{6,5},{7,6},{8,7},{9,8},{10,9... | collective-permute-start | bytes 1160 | tf_op jit(solution)/shard_map/ppermute | solution.py:12
  232.2 12.9 %collective-permute-start.8 = (bf16[2,8,64,64]{3,2,1,0:T(8,128)(2,1)S(1)}, bf16[2,8,64,64]{3,2,1,0:T(8,128)(2,1)S(1)}, u32[]{:S(2)}, u32[]{:S(2)}) collective-permute-start(bf16[2,8,64,64]{3,2,1,0:T(8,128)(2,1)S(1)} %collective-permute-done.3), channel_id=1, source_target_pairs={{0,31},{1,0},{2,1},{3,2},{4,3},{5,4},{6,5},{7,6},{8,7},{9,8},{10,9... | collective-permute-start | bytes 393224 | tf_op jit(solution)/shard_map/ppermute | solution.py:12
  245.1 1.9 collective-permute-start.7
  249.0 17.1 %collective-permute-start.9 = (bf16[2,8,64,64]{3,2,1,0:T(8,128)(2,1)S(1)}, bf16[2,8,64,64]{3,2,1,0:T(8,128)(2,1)S(1)}, u32[]{:S(2)}, u32[]{:S(2)}) collective-permute-start(bf16[2,8,64,64]{3,2,1,0:T(8,128)(2,1)S(1)} %collective-permute-done.8), channel_id=1, source_target_pairs={{0,32},{32,64},{64,96},{96,128},{128,160},{160,192},{192,224},{224... | collective-permute-start | bytes 393224 | tf_op jit(solution)/shard_map/ppermute | solution.py:12
  267.2 13.4 %collective-permute-start.14 = (bf16[2,8,64,64]{3,2,1,0:T(8,128)(2,1)S(1)}, bf16[2,8,64,64]{3,2,1,0:T(8,128)(2,1)S(1)}, u32[]{:S(2)}, u32[]{:S(2)}) collective-permute-start(bf16[2,8,64,64]{3,2,1,0:T(8,128)(2,1)S(1)} %collective-permute-done.9), channel_id=1, source_target_pairs={{0,31},{1,0},{2,1},{3,2},{4,3},{5,4},{6,5},{7,6},{8,7},{9,8},{10,9... | collective-permute-start | bytes 393224 | tf_op jit(solution)/shard_map/ppermute | solution.py:12
  280.9 9.9 %collective-permute-done.14 = bf16[2,8,64,64]{3,2,1,0:T(8,128)(2,1)S(1)} collective-permute-done((bf16[2,8,64,64]{3,2,1,0:T(8,128)(2,1)S(1)}, bf16[2,8,64,64]{3,2,1,0:T(8,128)(2,1)S(1)}, u32[]{:S(2)}, u32[]{:S(2)}) %collective-permute-start.14) | collective-permute-done | bytes 131104 | tf_op jit(solution)/shard_map/ppermute | solution.py:12
  290.8 17.4 %collective-permute-start.15 = (bf16[2,8,64,64]{3,2,1,0:T(8,128)(2,1)S(1)}, bf16[2,8,64,64]{3,2,1,0:T(8,128)(2,1)S(1)}, u32[]{:S(2)}, u32[]{:S(2)}) collective-permute-start(bf16[2,8,64,64]{3,2,1,0:T(8,128)(2,1)S(1)} %collective-permute-done.14), channel_id=1, source_target_pairs={{0,32},{32,64},{64,96},{96,128},{128,160},{160,192},{192,224},{224... | collective-permute-start | bytes 393224 | tf_op jit(solution)/shard_map/ppermute | solution.py:12
  309.4 12.8 %collective-permute-start.20 = (bf16[2,8,64,64]{3,2,1,0:T(8,128)(2,1)S(1)}, bf16[2,8,64,64]{3,2,1,0:T(8,128)(2,1)}, u32[]{:S(2)}, u32[]{:S(2)}) collective-permute-start(bf16[2,8,64,64]{3,2,1,0:T(8,128)(2,1)S(1)} %collective-permute-done.15), channel_id=1, source_target_pairs={{0,31},{1,0},{2,1},{3,2},{4,3},{5,4},{6,5},{7,6},{8,7},{9,8},{10,9... | collective-permute-start | bytes 393224 | tf_op jit(solution)/shard_map/ppermute | solution.py:12
  322.2 1.9 collective-permute-start.13
  329.6 24.4 %collective-permute-start.21 = (bf16[2,8,64,64]{3,2,1,0:T(8,128)(2,1)}, bf16[2,8,64,64]{3,2,1,0:T(8,128)(2,1)S(1)}, u32[]{:S(2)}, u32[]{:S(2)}) collective-permute-start(bf16[2,8,64,64]{3,2,1,0:T(8,128)(2,1)} %collective-permute-done.20), channel_id=1, source_target_pairs={{0,32},{32,64},{64,96},{96,128},{128,160},{160,192},{192,224},{224... | collective-permute-start | bytes 393224 | tf_op jit(solution)/shard_map/ppermute | solution.py:12
  355.7 11.0 %collective-permute-start.26 = (bf16[2,8,64,64]{3,2,1,0:T(8,128)(2,1)S(1)}, bf16[2,8,64,64]{3,2,1,0:T(8,128)(2,1)S(1)}, u32[]{:S(2)}, u32[]{:S(2)}) collective-permute-start(bf16[2,8,64,64]{3,2,1,0:T(8,128)(2,1)S(1)} %collective-permute-done.21), channel_id=1, source_target_pairs={{0,31},{1,0},{2,1},{3,2},{4,3},{5,4},{6,5},{7,6},{8,7},{9,8},{10,9... | collective-permute-start | bytes 393224 | tf_op jit(solution)/shard_map/ppermute | solution.py:12
  368.3 5.2 collective-permute-done.26
  373.6 22.1 %collective-permute-start.27 = (bf16[2,8,64,64]{3,2,1,0:T(8,128)(2,1)S(1)}, bf16[2,8,64,64]{3,2,1,0:T(8,128)(2,1)S(1)}, u32[]{:S(2)}, u32[]{:S(2)}) collective-permute-start(bf16[2,8,64,64]{3,2,1,0:T(8,128)(2,1)S(1)} %collective-permute-done.26), channel_id=1, source_target_pairs={{0,32},{32,64},{64,96},{96,128},{128,160},{160,192},{192,224},{224... | collective-permute-start | bytes 393224 | tf_op jit(solution)/shard_map/ppermute | solution.py:12
  397.4 12.8 %collective-permute-start.32 = (bf16[2,8,64,64]{3,2,1,0:T(8,128)(2,1)S(1)}, bf16[2,8,64,64]{3,2,1,0:T(8,128)(2,1)}, u32[]{:S(2)}, u32[]{:S(2)}) collective-permute-start(bf16[2,8,64,64]{3,2,1,0:T(8,128)(2,1)S(1)} %collective-permute-done.27), channel_id=1, source_target_pairs={{0,31},{1,0},{2,1},{3,2},{4,3},{5,4},{6,5},{7,6},{8,7},{9,8},{10,9... | collective-permute-start | bytes 393224 | tf_op jit(solution)/shard_map/ppermute | solution.py:12
  410.2 1.9 collective-permute-start.19
  413.8 5.0 collective-permute-done.32
  418.8 18.1 %collective-permute-start.33 = (bf16[2,8,64,64]{3,2,1,0:T(8,128)(2,1)}, bf16[2,8,64,64]{3,2,1,0:T(8,128)(2,1)S(1)}, u32[]{:S(2)}, u32[]{:S(2)}) collective-permute-start(bf16[2,8,64,64]{3,2,1,0:T(8,128)(2,1)} %collective-permute-done.32), channel_id=1, source_target_pairs={{0,32},{32,64},{64,96},{96,128},{128,160},{160,192},{192,224},{224... | collective-permute-start | bytes 393224 | tf_op jit(solution)/shard_map/ppermute | solution.py:12
  436.9 4.1 fusion.22
  441.0 3.3 copy.25
  444.4 13.5 %collective-permute-start.38 = (bf16[2,8,64,64]{3,2,1,0:T(8,128)(2,1)S(1)}, bf16[2,8,64,64]{3,2,1,0:T(8,128)(2,1)}, u32[]{:S(2)}, u32[]{:S(2)}) collective-permute-start(bf16[2,8,64,64]{3,2,1,0:T(8,128)(2,1)S(1)} %collective-permute-done.33), channel_id=1, source_target_pairs={{0,31},{1,0},{2,1},{3,2},{4,3},{5,4},{6,5},{7,6},{8,7},{9,8},{10,9... | collective-permute-start | bytes 393224 | tf_op jit(solution)/shard_map/ppermute | solution.py:12
  458.6 5.8 collective-permute-done.38
  464.4 18.1 %collective-permute-start.39 = (bf16[2,8,64,64]{3,2,1,0:T(8,128)(2,1)}, bf16[2,8,64,64]{3,2,1,0:T(8,128)(2,1)}, u32[]{:S(2)}, u32[]{:S(2)}) collective-permute-start(bf16[2,8,64,64]{3,2,1,0:T(8,128)(2,1)} %collective-permute-done.38), channel_id=1, source_target_pairs={{0,32},{32,64},{64,96},{96,128},{128,160},{160,192},{192,224},{224... | collective-permute-start | bytes 393224 | tf_op jit(solution)/shard_map/ppermute | solution.py:12
  482.6 12.9 %collective-permute-start.25 = (bf16[16,6,64,64]{3,2,1,0:T(8,128)(2,1)}, bf16[16,6,64,64]{3,2,1,0:T(8,128)(2,1)}, u32[]{:S(2)}, u32[]{:S(2)}) collective-permute-start(bf16[16,6,64,64]{3,2,1,0:T(8,128)(2,1)} %collective-permute-done.19), channel_id=1, source_target_pairs={{0,31},{1,0},{2,1},{3,2},{4,3},{5,4},{6,5},{7,6},{8,7},{9,8},{10,9... | collective-permute-start | bytes 2359304 | tf_op jit(solution)/shard_map/ppermute | solution.py:12
  495.5 4.1 fusion.20
  499.6 3.3 copy.30
  503.0 2.1 collective-permute-start.44
  506.7 37.5 %collective-permute-done.44 = bf16[2,8,64,64]{3,2,1,0:T(8,128)(2,1)} collective-permute-done((bf16[2,8,64,64]{3,2,1,0:T(8,128)(2,1)}, bf16[2,8,64,64]{3,2,1,0:T(8,128)(2,1)}, u32[]{:S(2)}, u32[]{:S(2)}) %collective-permute-start.44) | collective-permute-done | bytes 131104 | tf_op jit(solution)/shard_map/ppermute | solution.py:12
  544.1 5.5 collective-permute-start.45
  549.6 4.1 fusion.18
  553.8 3.3 copy.35
  557.1 13.0 %collective-permute-start.31 = (bf16[16,6,64,64]{3,2,1,0:T(8,128)(2,1)}, bf16[16,6,64,64]{3,2,1,0:T(8,128)(2,1)}, u32[]{:S(2)}, u32[]{:S(2)}) collective-permute-start(bf16[16,6,64,64]{3,2,1,0:T(8,128)(2,1)} %collective-permute-done.25), channel_id=1, source_target_pairs={{0,31},{1,0},{2,1},{3,2},{4,3},{5,4},{6,5},{7,6},{8,7},{9,8},{10,9... | collective-permute-start | bytes 2359304 | tf_op jit(solution)/shard_map/ppermute | solution.py:12
  571.6 4.1 fusion.16
  575.8 3.4 copy.40
  579.9 24.4 %collective-permute-done.31 = bf16[16,6,64,64]{3,2,1,0:T(8,128)(2,1)} collective-permute-done((bf16[16,6,64,64]{3,2,1,0:T(8,128)(2,1)}, bf16[16,6,64,64]{3,2,1,0:T(8,128)(2,1)}, u32[]{:S(2)}, u32[]{:S(2)}) %collective-permute-start.31) | collective-permute-done | bytes 786464 | tf_op jit(solution)/shard_map/ppermute | solution.py:12
  604.3 13.1 %collective-permute-start.37 = (bf16[16,6,64,64]{3,2,1,0:T(8,128)(2,1)}, bf16[16,6,64,64]{3,2,1,0:T(8,128)(2,1)}, u32[]{:S(2)}, u32[]{:S(2)}) collective-permute-start(bf16[16,6,64,64]{3,2,1,0:T(8,128)(2,1)} %collective-permute-done.31), channel_id=1, source_target_pairs={{0,31},{1,0},{2,1},{3,2},{4,3},{5,4},{6,5},{7,6},{8,7},{9,8},{10,9... | collective-permute-start | bytes 2359304 | tf_op jit(solution)/shard_map/ppermute | solution.py:12
  617.4 4.1 fusion.14
  621.5 3.3 copy.45
  625.8 4.1 fusion.12
  629.9 3.3 copy.50
  633.3 17.4 %collective-permute-done.37 = bf16[16,6,64,64]{3,2,1,0:T(8,128)(2,1)} collective-permute-done((bf16[16,6,64,64]{3,2,1,0:T(8,128)(2,1)}, bf16[16,6,64,64]{3,2,1,0:T(8,128)(2,1)}, u32[]{:S(2)}, u32[]{:S(2)}) %collective-permute-start.37) | collective-permute-done | bytes 786464 | tf_op jit(solution)/shard_map/ppermute | solution.py:12
  650.6 13.3 %collective-permute-start.43 = (bf16[16,6,64,64]{3,2,1,0:T(8,128)(2,1)}, bf16[16,6,64,64]{3,2,1,0:T(8,128)(2,1)}, u32[]{:S(2)}, u32[]{:S(2)}) collective-permute-start(bf16[16,6,64,64]{3,2,1,0:T(8,128)(2,1)} %collective-permute-done.37), channel_id=1, source_target_pairs={{0,31},{1,0},{2,1},{3,2},{4,3},{5,4},{6,5},{7,6},{8,7},{9,8},{10,9... | collective-permute-start | bytes 2359304 | tf_op jit(solution)/shard_map/ppermute | solution.py:12
  664.7 4.1 fusion.10
  668.8 3.3 copy.55
  673.8 22.3 %collective-permute-done.43 = bf16[16,6,64,64]{3,2,1,0:T(8,128)(2,1)} collective-permute-done((bf16[16,6,64,64]{3,2,1,0:T(8,128)(2,1)}, bf16[16,6,64,64]{3,2,1,0:T(8,128)(2,1)}, u32[]{:S(2)}, u32[]{:S(2)}) %collective-permute-start.43) | collective-permute-done | bytes 786464 | tf_op jit(solution)/shard_map/ppermute | solution.py:12
  696.1 4.1 fusion.8
  700.2 3.3 copy.60
  (127 shorter events, 47.9 us)
Async XLA Ops:
  0.0 14.6 %collective-permute-start.1 = (s32[2,8]{1,0:T(2,128)}, s32[2,8]{1,0:T(2,128)S(1)}, u32[]{:S(2)}, u32[]{:S(2)}) collective-permute-start(s32[2,8]{1,0:T(2,128)} %bitcast.231), channel_id=1, source_target_pairs={{0,7},{1,8},{2,9},{3,10},{4,11},{5,12},{6,13},{7,14},{8,15},{9,16}... | collective-permute-start | bytes 200 | tf_op jit(solution)/shard_map/ppermute | solution.py:12
  14.6 14.9 %collective-permute-start.5 = (s32[2,8]{1,0:T(2,128)S(1)}, s32[2,8]{1,0:T(2,128)S(1)}, u32[]{:S(2)}, u32[]{:S(2)}) collective-permute-start(s32[2,8]{1,0:T(2,128)S(1)} %collective-permute-done.1), channel_id=1, source_target_pairs={{0,31},{1,0},{2,1},{3,2},{4,3},{5,4},{6,5},{7,6},{8,7},{9,8},{10,9... | collective-permute-start | bytes 200 | tf_op jit(solution)/shard_map/ppermute | solution.py:12
  27.6 66.2 %collective-permute-start = (s32[16,6]{0,1:T(8,128)S(1)}, s32[16,6]{0,1:T(8,128)S(1)}, u32[]{:S(2)}, u32[]{:S(2)}) collective-permute-start(s32[16,6]{0,1:T(8,128)S(1)} %bitcast.227), channel_id=1, source_target_pairs={{0,7},{1,8},{2,9},{3,10},{4,11},{5,12},{6,13},{7,14},{8,15},{9,16}... | collective-permute-start | bytes 1160 | tf_op jit(solution)/shard_map/ppermute | solution.py:12
  29.6 10.8 %collective-permute-start.6 = (s32[2,8]{1,0:T(2,128)S(1)}, s32[2,8]{1,0:T(2,128)S(1)}, u32[]{:S(2)}, u32[]{:S(2)}) collective-permute-start(s32[2,8]{1,0:T(2,128)S(1)} %collective-permute-done.5), channel_id=1, source_target_pairs={{0,32},{32,64},{64,96},{96,128},{128,160},{160,192},{192,224},{224... | collective-permute-start | bytes 200 | tf_op jit(solution)/shard_map/ppermute | solution.py:12
  31.5 213.6 %collective-permute-start.2 = (bf16[16,6,64,64]{3,2,1,0:T(8,128)(2,1)}, bf16[16,6,64,64]{3,2,1,0:T(8,128)(2,1)}, u32[]{:S(2)}, u32[]{:S(2)}) collective-permute-start(bf16[16,6,64,64]{3,2,1,0:T(8,128)(2,1)} %bitcast.229), channel_id=1, source_target_pairs={{0,7},{1,8},{2,9},{3,10},{4,11},{5,12},{6,13},{7,14},{8,15},{9,16}... | collective-permute-start | bytes 2359304 | tf_op jit(solution)/shard_map/ppermute | solution.py:12
  40.3 29.9 %collective-permute-start.11 = (s32[2,8]{1,0:T(2,128)S(1)}, s32[2,8]{1,0:T(2,128)S(1)}, u32[]{:S(2)}, u32[]{:S(2)}) collective-permute-start(s32[2,8]{1,0:T(2,128)S(1)} %collective-permute-done.6), channel_id=1, source_target_pairs={{0,31},{1,0},{2,1},{3,2},{4,3},{5,4},{6,5},{7,6},{8,7},{9,8},{10,9... | collective-permute-start | bytes 200 | tf_op jit(solution)/shard_map/ppermute | solution.py:12
  46.7 185.6 %collective-permute-start.3 = (bf16[2,8,64,64]{3,2,1,0:T(8,128)(2,1)}, bf16[2,8,64,64]{3,2,1,0:T(8,128)(2,1)S(1)}, u32[]{:S(2)}, u32[]{:S(2)}) collective-permute-start(bf16[2,8,64,64]{3,2,1,0:T(8,128)(2,1)} %bitcast.230), channel_id=1, source_target_pairs={{0,7},{1,8},{2,9},{3,10},{4,11},{5,12},{6,13},{7,14},{8,15},{9,16}... | collective-permute-start | bytes 393224 | tf_op jit(solution)/shard_map/ppermute | solution.py:12
  70.2 10.8 %collective-permute-start.12 = (s32[2,8]{1,0:T(2,128)S(1)}, s32[2,8]{1,0:T(2,128)S(1)}, u32[]{:S(2)}, u32[]{:S(2)}) collective-permute-start(s32[2,8]{1,0:T(2,128)S(1)} %collective-permute-done.11), channel_id=1, source_target_pairs={{0,32},{32,64},{64,96},{96,128},{128,160},{160,192},{192,224},{224... | collective-permute-start | bytes 200 | tf_op jit(solution)/shard_map/ppermute | solution.py:12
  81.0 14.7 %collective-permute-start.17 = (s32[2,8]{1,0:T(2,128)S(1)}, s32[2,8]{1,0:T(2,128)S(1)}, u32[]{:S(2)}, u32[]{:S(2)}) collective-permute-start(s32[2,8]{1,0:T(2,128)S(1)} %collective-permute-done.12), channel_id=1, source_target_pairs={{0,31},{1,0},{2,1},{3,2},{4,3},{5,4},{6,5},{7,6},{8,7},{9,8},{10,9... | collective-permute-start | bytes 200 | tf_op jit(solution)/shard_map/ppermute | solution.py:12
  93.8 19.0 %collective-permute-start.4 = (s32[16,6]{0,1:T(8,128)S(1)}, s32[16,6]{0,1:T(8,128)S(1)}, u32[]{:S(2)}, u32[]{:S(2)}) collective-permute-start(s32[16,6]{0,1:T(8,128)S(1)} %collective-permute-done), channel_id=1, source_target_pairs={{0,31},{1,0},{2,1},{3,2},{4,3},{5,4},{6,5},{7,6},{8,7},{9,8},{10,9... | collective-permute-start | bytes 1160 | tf_op jit(solution)/shard_map/ppermute | solution.py:12
  95.7 5.1 collective-permute-start.18
  100.8 14.0 %collective-permute-start.23 = (s32[2,8]{1,0:T(2,128)S(1)}, s32[2,8]{1,0:T(2,128)S(1)}, u32[]{:S(2)}, u32[]{:S(2)}) collective-permute-start(s32[2,8]{1,0:T(2,128)S(1)} %collective-permute-done.18), channel_id=1, source_target_pairs={{0,31},{1,0},{2,1},{3,2},{4,3},{5,4},{6,5},{7,6},{8,7},{9,8},{10,9... | collective-permute-start | bytes 200 | tf_op jit(solution)/shard_map/ppermute | solution.py:12
  112.8 29.2 %collective-permute-start.10 = (s32[16,6]{0,1:T(8,128)S(1)}, s32[16,6]{0,1:T(8,128)S(1)}, u32[]{:S(2)}, u32[]{:S(2)}) collective-permute-start(s32[16,6]{0,1:T(8,128)S(1)} %collective-permute-done.4), channel_id=1, source_target_pairs={{0,31},{1,0},{2,1},{3,2},{4,3},{5,4},{6,5},{7,6},{8,7},{9,8},{10,9... | collective-permute-start | bytes 1160 | tf_op jit(solution)/shard_map/ppermute | solution.py:12
  114.8 15.9 %collective-permute-start.24 = (s32[2,8]{1,0:T(2,128)S(1)}, s32[2,8]{1,0:T(2,128)S(1)}, u32[]{:S(2)}, u32[]{:S(2)}) collective-permute-start(s32[2,8]{1,0:T(2,128)S(1)} %collective-permute-done.23), channel_id=1, source_target_pairs={{0,32},{32,64},{64,96},{96,128},{128,160},{160,192},{192,224},{224... | collective-permute-start | bytes 200 | tf_op jit(solution)/shard_map/ppermute | solution.py:12
  130.7 13.3 %collective-permute-start.29 = (s32[2,8]{1,0:T(2,128)S(1)}, s32[2,8]{1,0:T(2,128)S(1)}, u32[]{:S(2)}, u32[]{:S(2)}) collective-permute-start(s32[2,8]{1,0:T(2,128)S(1)} %collective-permute-done.24), channel_id=1, source_target_pairs={{0,31},{1,0},{2,1},{3,2},{4,3},{5,4},{6,5},{7,6},{8,7},{9,8},{10,9... | collective-permute-start | bytes 200 | tf_op jit(solution)/shard_map/ppermute | solution.py:12
  142.0 17.7 %collective-permute-start.16 = (s32[16,6]{0,1:T(8,128)S(1)}, s32[16,6]{0,1:T(8,128)S(1)}, u32[]{:S(2)}, u32[]{:S(2)}) collective-permute-start(s32[16,6]{0,1:T(8,128)S(1)} %collective-permute-done.10), channel_id=1, source_target_pairs={{0,31},{1,0},{2,1},{3,2},{4,3},{5,4},{6,5},{7,6},{8,7},{9,8},{10,9... | collective-permute-start | bytes 1160 | tf_op jit(solution)/shard_map/ppermute | solution.py:12
  144.0 27.1 %collective-permute-start.30 = (s32[2,8]{1,0:T(2,128)S(1)}, s32[2,8]{1,0:T(2,128)S(1)}, u32[]{:S(2)}, u32[]{:S(2)}) collective-permute-start(s32[2,8]{1,0:T(2,128)S(1)} %collective-permute-done.29), channel_id=1, source_target_pairs={{0,32},{32,64},{64,96},{96,128},{128,160},{160,192},{192,224},{224... | collective-permute-start | bytes 200 | tf_op jit(solution)/shard_map/ppermute | solution.py:12
  159.8 13.3 %collective-permute-start.22 = (s32[16,6]{0,1:T(8,128)S(1)}, s32[16,6]{0,1:T(8,128)S(1)}, u32[]{:S(2)}, u32[]{:S(2)}) collective-permute-start(s32[16,6]{0,1:T(8,128)S(1)} %collective-permute-done.16), channel_id=1, source_target_pairs={{0,31},{1,0},{2,1},{3,2},{4,3},{5,4},{6,5},{7,6},{8,7},{9,8},{10,9... | collective-permute-start | bytes 1160 | tf_op jit(solution)/shard_map/ppermute | solution.py:12
  171.1 14.2 %collective-permute-start.35 = (s32[2,8]{1,0:T(2,128)S(1)}, s32[2,8]{1,0:T(2,128)S(1)}, u32[]{:S(2)}, u32[]{:S(2)}) collective-permute-start(s32[2,8]{1,0:T(2,128)S(1)} %collective-permute-done.30), channel_id=1, source_target_pairs={{0,31},{1,0},{2,1},{3,2},{4,3},{5,4},{6,5},{7,6},{8,7},{9,8},{10,9... | collective-permute-start | bytes 200 | tf_op jit(solution)/shard_map/ppermute | solution.py:12
  173.1 30.0 %collective-permute-start.28 = (s32[16,6]{0,1:T(8,128)S(1)}, s32[16,6]{0,1:T(8,128)S(1)}, u32[]{:S(2)}, u32[]{:S(2)}) collective-permute-start(s32[16,6]{0,1:T(8,128)S(1)} %collective-permute-done.22), channel_id=1, source_target_pairs={{0,31},{1,0},{2,1},{3,2},{4,3},{5,4},{6,5},{7,6},{8,7},{9,8},{10,9... | collective-permute-start | bytes 1160 | tf_op jit(solution)/shard_map/ppermute | solution.py:12
  185.3 15.5 %collective-permute-start.36 = (s32[2,8]{1,0:T(2,128)S(1)}, s32[2,8]{1,0:T(2,128)S(1)}, u32[]{:S(2)}, u32[]{:S(2)}) collective-permute-start(s32[2,8]{1,0:T(2,128)S(1)} %collective-permute-done.35), channel_id=1, source_target_pairs={{0,32},{32,64},{64,96},{96,128},{128,160},{160,192},{192,224},{224... | collective-permute-start | bytes 200 | tf_op jit(solution)/shard_map/ppermute | solution.py:12
  200.9 5.5 collective-permute-start.41
  203.1 16.4 %collective-permute-start.34 = (s32[16,6]{0,1:T(8,128)S(1)}, s32[16,6]{0,1:T(8,128)S(1)}, u32[]{:S(2)}, u32[]{:S(2)}) collective-permute-start(s32[16,6]{0,1:T(8,128)S(1)} %collective-permute-done.28), channel_id=1, source_target_pairs={{0,31},{1,0},{2,1},{3,2},{4,3},{5,4},{6,5},{7,6},{8,7},{9,8},{10,9... | collective-permute-start | bytes 1160 | tf_op jit(solution)/shard_map/ppermute | solution.py:12
  206.3 24.5 %collective-permute-start.42 = (s32[2,8]{1,0:T(2,128)S(1)}, s32[2,8]{1,0:T(2,128)S(1)}, u32[]{:S(2)}, u32[]{:S(2)}) collective-permute-start(s32[2,8]{1,0:T(2,128)S(1)} %collective-permute-done.41), channel_id=1, source_target_pairs={{0,32},{32,64},{64,96},{96,128},{128,160},{160,192},{192,224},{224... | collective-permute-start | bytes 200 | tf_op jit(solution)/shard_map/ppermute | solution.py:12
  219.5 12.6 %collective-permute-start.40 = (s32[16,6]{0,1:T(8,128)S(1)}, s32[16,6]{0,1:T(8,128)S(1)}, u32[]{:S(2)}, u32[]{:S(2)}) collective-permute-start(s32[16,6]{0,1:T(8,128)S(1)} %collective-permute-done.34), channel_id=1, source_target_pairs={{0,31},{1,0},{2,1},{3,2},{4,3},{5,4},{6,5},{7,6},{8,7},{9,8},{10,9... | collective-permute-start | bytes 1160 | tf_op jit(solution)/shard_map/ppermute | solution.py:12
  232.2 16.8 %collective-permute-start.8 = (bf16[2,8,64,64]{3,2,1,0:T(8,128)(2,1)S(1)}, bf16[2,8,64,64]{3,2,1,0:T(8,128)(2,1)S(1)}, u32[]{:S(2)}, u32[]{:S(2)}) collective-permute-start(bf16[2,8,64,64]{3,2,1,0:T(8,128)(2,1)S(1)} %collective-permute-done.3), channel_id=1, source_target_pairs={{0,31},{1,0},{2,1},{3,2},{4,3},{5,4},{6,5},{7,6},{8,7},{9,8},{10,9... | collective-permute-start | bytes 393224 | tf_op jit(solution)/shard_map/ppermute | solution.py:12
  245.1 77.1 %collective-permute-start.7 = (bf16[16,6,64,64]{3,2,1,0:T(8,128)(2,1)}, bf16[16,6,64,64]{3,2,1,0:T(8,128)(2,1)}, u32[]{:S(2)}, u32[]{:S(2)}) collective-permute-start(bf16[16,6,64,64]{3,2,1,0:T(8,128)(2,1)} %collective-permute-done.2), channel_id=1, source_target_pairs={{0,31},{1,0},{2,1},{3,2},{4,3},{5,4},{6,5},{7,6},{8,7},{9,8},{10,9... | collective-permute-start | bytes 2359304 | tf_op jit(solution)/shard_map/ppermute | solution.py:12
  249.0 18.2 %collective-permute-start.9 = (bf16[2,8,64,64]{3,2,1,0:T(8,128)(2,1)S(1)}, bf16[2,8,64,64]{3,2,1,0:T(8,128)(2,1)S(1)}, u32[]{:S(2)}, u32[]{:S(2)}) collective-permute-start(bf16[2,8,64,64]{3,2,1,0:T(8,128)(2,1)S(1)} %collective-permute-done.8), channel_id=1, source_target_pairs={{0,32},{32,64},{64,96},{96,128},{128,160},{160,192},{192,224},{224... | collective-permute-start | bytes 393224 | tf_op jit(solution)/shard_map/ppermute | solution.py:12
  267.2 23.6 %copy-start.1 = (bf16[2,8,64,64]{3,2,1,0:T(8,128)(2,1)}, bf16[2,8,64,64]{3,2,1,0:T(8,128)(2,1)S(1)}, u32[]{:S(2)}) copy-start(bf16[2,8,64,64]{3,2,1,0:T(8,128)(2,1)S(1)} %collective-permute-done.9) | copy-start | bytes 393220
  267.2 23.6 %collective-permute-start.14 = (bf16[2,8,64,64]{3,2,1,0:T(8,128)(2,1)S(1)}, bf16[2,8,64,64]{3,2,1,0:T(8,128)(2,1)S(1)}, u32[]{:S(2)}, u32[]{:S(2)}) collective-permute-start(bf16[2,8,64,64]{3,2,1,0:T(8,128)(2,1)S(1)} %collective-permute-done.9), channel_id=1, source_target_pairs={{0,31},{1,0},{2,1},{3,2},{4,3},{5,4},{6,5},{7,6},{8,7},{9,8},{10,9... | collective-permute-start | bytes 393224 | tf_op jit(solution)/shard_map/ppermute | solution.py:12
  290.8 18.6 %collective-permute-start.15 = (bf16[2,8,64,64]{3,2,1,0:T(8,128)(2,1)S(1)}, bf16[2,8,64,64]{3,2,1,0:T(8,128)(2,1)S(1)}, u32[]{:S(2)}, u32[]{:S(2)}) collective-permute-start(bf16[2,8,64,64]{3,2,1,0:T(8,128)(2,1)S(1)} %collective-permute-done.14), channel_id=1, source_target_pairs={{0,32},{32,64},{64,96},{96,128},{128,160},{160,192},{192,224},{224... | collective-permute-start | bytes 393224 | tf_op jit(solution)/shard_map/ppermute | solution.py:12
  309.4 20.2 %collective-permute-start.20 = (bf16[2,8,64,64]{3,2,1,0:T(8,128)(2,1)S(1)}, bf16[2,8,64,64]{3,2,1,0:T(8,128)(2,1)}, u32[]{:S(2)}, u32[]{:S(2)}) collective-permute-start(bf16[2,8,64,64]{3,2,1,0:T(8,128)(2,1)S(1)} %collective-permute-done.15), channel_id=1, source_target_pairs={{0,31},{1,0},{2,1},{3,2},{4,3},{5,4},{6,5},{7,6},{8,7},{9,8},{10,9... | collective-permute-start | bytes 393224 | tf_op jit(solution)/shard_map/ppermute | solution.py:12
  322.2 88.0 %collective-permute-start.13 = (bf16[16,6,64,64]{3,2,1,0:T(8,128)(2,1)}, bf16[16,6,64,64]{3,2,1,0:T(8,128)(2,1)}, u32[]{:S(2)}, u32[]{:S(2)}) collective-permute-start(bf16[16,6,64,64]{3,2,1,0:T(8,128)(2,1)} %collective-permute-done.7), channel_id=1, source_target_pairs={{0,31},{1,0},{2,1},{3,2},{4,3},{5,4},{6,5},{7,6},{8,7},{9,8},{10,9... | collective-permute-start | bytes 2359304 | tf_op jit(solution)/shard_map/ppermute | solution.py:12
  329.6 26.1 %collective-permute-start.21 = (bf16[2,8,64,64]{3,2,1,0:T(8,128)(2,1)}, bf16[2,8,64,64]{3,2,1,0:T(8,128)(2,1)S(1)}, u32[]{:S(2)}, u32[]{:S(2)}) collective-permute-start(bf16[2,8,64,64]{3,2,1,0:T(8,128)(2,1)} %collective-permute-done.20), channel_id=1, source_target_pairs={{0,32},{32,64},{64,96},{96,128},{128,160},{160,192},{192,224},{224... | collective-permute-start | bytes 393224 | tf_op jit(solution)/shard_map/ppermute | solution.py:12
  355.7 58.1 %copy-start.2 = (bf16[2,8,64,64]{3,2,1,0:T(8,128)(2,1)}, bf16[2,8,64,64]{3,2,1,0:T(8,128)(2,1)S(1)}, u32[]{:S(2)}) copy-start(bf16[2,8,64,64]{3,2,1,0:T(8,128)(2,1)S(1)} %collective-permute-done.21) | copy-start | bytes 393220
  355.7 17.9 %collective-permute-start.26 = (bf16[2,8,64,64]{3,2,1,0:T(8,128)(2,1)S(1)}, bf16[2,8,64,64]{3,2,1,0:T(8,128)(2,1)S(1)}, u32[]{:S(2)}, u32[]{:S(2)}) collective-permute-start(bf16[2,8,64,64]{3,2,1,0:T(8,128)(2,1)S(1)} %collective-permute-done.21), channel_id=1, source_target_pairs={{0,31},{1,0},{2,1},{3,2},{4,3},{5,4},{6,5},{7,6},{8,7},{9,8},{10,9... | collective-permute-start | bytes 393224 | tf_op jit(solution)/shard_map/ppermute | solution.py:12
  367.0 69.8 %copy-start.15 = (bf16[2,8,8,16,6,1]{3,2,4,5,1,0:T(8,128)(2,1)S(1)}, bf16[2,8,8,16,6,1]{3,2,4,5,1,0:T(8,128)(2,1)}, u32[]{:S(2)}) copy-start(bf16[2,8,8,16,6,1]{3,2,4,5,1,0:T(8,128)(2,1)} %copy.23) | copy-start | bytes 73732
  373.6 23.8 %collective-permute-start.27 = (bf16[2,8,64,64]{3,2,1,0:T(8,128)(2,1)S(1)}, bf16[2,8,64,64]{3,2,1,0:T(8,128)(2,1)S(1)}, u32[]{:S(2)}, u32[]{:S(2)}) collective-permute-start(bf16[2,8,64,64]{3,2,1,0:T(8,128)(2,1)S(1)} %collective-permute-done.26), channel_id=1, source_target_pairs={{0,32},{32,64},{64,96},{96,128},{128,160},{160,192},{192,224},{224... | collective-permute-start | bytes 393224 | tf_op jit(solution)/shard_map/ppermute | solution.py:12
  397.4 43.6 %copy-start.4 = (bf16[2,8,64,64]{3,2,1,0:T(8,128)(2,1)}, bf16[2,8,64,64]{3,2,1,0:T(8,128)(2,1)S(1)}, u32[]{:S(2)}) copy-start(bf16[2,8,64,64]{3,2,1,0:T(8,128)(2,1)S(1)} %collective-permute-done.27) | copy-start | bytes 393220
  397.4 21.4 %collective-permute-start.32 = (bf16[2,8,64,64]{3,2,1,0:T(8,128)(2,1)S(1)}, bf16[2,8,64,64]{3,2,1,0:T(8,128)(2,1)}, u32[]{:S(2)}, u32[]{:S(2)}) collective-permute-start(bf16[2,8,64,64]{3,2,1,0:T(8,128)(2,1)S(1)} %collective-permute-done.27), channel_id=1, source_target_pairs={{0,31},{1,0},{2,1},{3,2},{4,3},{5,4},{6,5},{7,6},{8,7},{9,8},{10,9... | collective-permute-start | bytes 393224 | tf_op jit(solution)/shard_map/ppermute | solution.py:12
  410.2 72.3 %collective-permute-start.19 = (bf16[16,6,64,64]{3,2,1,0:T(8,128)(2,1)}, bf16[16,6,64,64]{3,2,1,0:T(8,128)(2,1)}, u32[]{:S(2)}, u32[]{:S(2)}) collective-permute-start(bf16[16,6,64,64]{3,2,1,0:T(8,128)(2,1)} %collective-permute-done.13), channel_id=1, source_target_pairs={{0,31},{1,0},{2,1},{3,2},{4,3},{5,4},{6,5},{7,6},{8,7},{9,8},{10,9... | collective-permute-start | bytes 2359304 | tf_op jit(solution)/shard_map/ppermute | solution.py:12
  418.8 25.6 %collective-permute-start.33 = (bf16[2,8,64,64]{3,2,1,0:T(8,128)(2,1)}, bf16[2,8,64,64]{3,2,1,0:T(8,128)(2,1)S(1)}, u32[]{:S(2)}, u32[]{:S(2)}) collective-permute-start(bf16[2,8,64,64]{3,2,1,0:T(8,128)(2,1)} %collective-permute-done.32), channel_id=1, source_target_pairs={{0,32},{32,64},{64,96},{96,128},{128,160},{160,192},{192,224},{224... | collective-permute-start | bytes 393224 | tf_op jit(solution)/shard_map/ppermute | solution.py:12
  444.3 51.2 %copy-start.14 = (bf16[2,8,8,16,6,1]{3,2,4,5,1,0:T(8,128)(2,1)S(1)}, bf16[2,8,8,16,6,1]{3,2,4,5,1,0:T(8,128)(2,1)}, u32[]{:S(2)}) copy-start(bf16[2,8,8,16,6,1]{3,2,4,5,1,0:T(8,128)(2,1)} %copy.28) | copy-start | bytes 73732
  444.3 55.3 %copy-start.6 = (bf16[2,8,64,64]{3,2,1,0:T(8,128)(2,1)}, bf16[2,8,64,64]{3,2,1,0:T(8,128)(2,1)S(1)}, u32[]{:S(2)}) copy-start(bf16[2,8,64,64]{3,2,1,0:T(8,128)(2,1)S(1)} %collective-permute-done.33) | copy-start | bytes 393220
  444.4 20.1 %collective-permute-start.38 = (bf16[2,8,64,64]{3,2,1,0:T(8,128)(2,1)S(1)}, bf16[2,8,64,64]{3,2,1,0:T(8,128)(2,1)}, u32[]{:S(2)}, u32[]{:S(2)}) collective-permute-start(bf16[2,8,64,64]{3,2,1,0:T(8,128)(2,1)S(1)} %collective-permute-done.33), channel_id=1, source_target_pairs={{0,31},{1,0},{2,1},{3,2},{4,3},{5,4},{6,5},{7,6},{8,7},{9,8},{10,9... | collective-permute-start | bytes 393224 | tf_op jit(solution)/shard_map/ppermute | solution.py:12
  464.4 38.5 %collective-permute-start.39 = (bf16[2,8,64,64]{3,2,1,0:T(8,128)(2,1)}, bf16[2,8,64,64]{3,2,1,0:T(8,128)(2,1)}, u32[]{:S(2)}, u32[]{:S(2)}) collective-permute-start(bf16[2,8,64,64]{3,2,1,0:T(8,128)(2,1)} %collective-permute-done.38), channel_id=1, source_target_pairs={{0,32},{32,64},{64,96},{96,128},{128,160},{160,192},{192,224},{224... | collective-permute-start | bytes 393224 | tf_op jit(solution)/shard_map/ppermute | solution.py:12
  482.6 74.5 %collective-permute-start.25 = (bf16[16,6,64,64]{3,2,1,0:T(8,128)(2,1)}, bf16[16,6,64,64]{3,2,1,0:T(8,128)(2,1)}, u32[]{:S(2)}, u32[]{:S(2)}) collective-permute-start(bf16[16,6,64,64]{3,2,1,0:T(8,128)(2,1)} %collective-permute-done.19), channel_id=1, source_target_pairs={{0,31},{1,0},{2,1},{3,2},{4,3},{5,4},{6,5},{7,6},{8,7},{9,8},{10,9... | collective-permute-start | bytes 2359304 | tf_op jit(solution)/shard_map/ppermute | solution.py:12
  502.9 46.7 %copy-start.12 = (bf16[2,8,8,16,6,1]{3,2,4,5,1,0:T(8,128)(2,1)S(1)}, bf16[2,8,8,16,6,1]{3,2,4,5,1,0:T(8,128)(2,1)}, u32[]{:S(2)}) copy-start(bf16[2,8,8,16,6,1]{3,2,4,5,1,0:T(8,128)(2,1)} %copy.33) | copy-start | bytes 73732
  503.0 41.2 %collective-permute-start.44 = (bf16[2,8,64,64]{3,2,1,0:T(8,128)(2,1)}, bf16[2,8,64,64]{3,2,1,0:T(8,128)(2,1)}, u32[]{:S(2)}, u32[]{:S(2)}) collective-permute-start(bf16[2,8,64,64]{3,2,1,0:T(8,128)(2,1)} %collective-permute-done.39), channel_id=1, source_target_pairs={{0,31},{1,0},{2,1},{3,2},{4,3},{5,4},{6,5},{7,6},{8,7},{9,8},{10,9... | collective-permute-start | bytes 393224 | tf_op jit(solution)/shard_map/ppermute | solution.py:12
  544.1 159.4 %collective-permute-start.45 = (bf16[2,8,64,64]{3,2,1,0:T(8,128)(2,1)}, bf16[2,8,64,64]{3,2,1,0:T(8,128)(2,1)}, u32[]{:S(2)}, u32[]{:S(2)}) collective-permute-start(bf16[2,8,64,64]{3,2,1,0:T(8,128)(2,1)} %collective-permute-done.44), channel_id=1, source_target_pairs={{0,32},{32,64},{64,96},{96,128},{128,160},{160,192},{192,224},{224... | collective-permute-start | bytes 393224 | tf_op jit(solution)/shard_map/ppermute | solution.py:12
  557.1 14.6 %copy-start.9 = (bf16[2,8,8,16,6,1]{3,2,4,5,1,0:T(8,128)(2,1)S(1)}, bf16[2,8,8,16,6,1]{3,2,4,5,1,0:T(8,128)(2,1)}, u32[]{:S(2)}) copy-start(bf16[2,8,8,16,6,1]{3,2,4,5,1,0:T(8,128)(2,1)} %copy.38) | copy-start | bytes 73732
  557.1 47.2 %collective-permute-start.31 = (bf16[16,6,64,64]{3,2,1,0:T(8,128)(2,1)}, bf16[16,6,64,64]{3,2,1,0:T(8,128)(2,1)}, u32[]{:S(2)}, u32[]{:S(2)}) collective-permute-start(bf16[16,6,64,64]{3,2,1,0:T(8,128)(2,1)} %collective-permute-done.25), channel_id=1, source_target_pairs={{0,31},{1,0},{2,1},{3,2},{4,3},{5,4},{6,5},{7,6},{8,7},{9,8},{10,9... | collective-permute-start | bytes 2359304 | tf_op jit(solution)/shard_map/ppermute | solution.py:12
  575.8 3.4 copy-start
  575.8 3.4 copy-start.3
  579.2 38.2 %copy-start.8 = (bf16[2,8,8,16,6,1]{3,2,4,5,1,0:T(8,128)(2,1)S(1)}, bf16[2,8,8,16,6,1]{3,2,4,5,1,0:T(8,128)(2,1)}, u32[]{:S(2)}) copy-start(bf16[2,8,8,16,6,1]{3,2,4,5,1,0:T(8,128)(2,1)} %copy.43) | copy-start | bytes 73732
  604.3 46.4 %collective-permute-start.37 = (bf16[16,6,64,64]{3,2,1,0:T(8,128)(2,1)}, bf16[16,6,64,64]{3,2,1,0:T(8,128)(2,1)}, u32[]{:S(2)}, u32[]{:S(2)}) collective-permute-start(bf16[16,6,64,64]{3,2,1,0:T(8,128)(2,1)} %collective-permute-done.31), channel_id=1, source_target_pairs={{0,31},{1,0},{2,1},{3,2},{4,3},{5,4},{6,5},{7,6},{8,7},{9,8},{10,9... | collective-permute-start | bytes 2359304 | tf_op jit(solution)/shard_map/ppermute | solution.py:12
  621.5 3.3 copy-start.5
  624.9 0.9 copy-start.11
  629.9 34.0 %copy-start.7 = (bf16[2,8,64,64]{3,2,1,0:T(8,128)(2,1)S(1)}, bf16[2,8,64,64]{3,2,1,0:T(8,128)(2,1)}, u32[]{:S(2)}) copy-start(bf16[2,8,64,64]{3,2,1,0:T(8,128)(2,1)} %copy-done.6) | copy-start | bytes 393220
  633.3 31.4 %copy-start.10 = (bf16[2,8,8,16,6,1]{3,2,4,5,1,0:T(8,128)(2,1)S(1)}, bf16[2,8,8,16,6,1]{3,2,4,5,1,0:T(8,128)(2,1)}, u32[]{:S(2)}) copy-start(bf16[2,8,8,16,6,1]{3,2,4,5,1,0:T(8,128)(2,1)} %copy.53) | copy-start | bytes 73732
  650.6 45.5 %collective-permute-start.43 = (bf16[16,6,64,64]{3,2,1,0:T(8,128)(2,1)}, bf16[16,6,64,64]{3,2,1,0:T(8,128)(2,1)}, u32[]{:S(2)}, u32[]{:S(2)}) collective-permute-start(bf16[16,6,64,64]{3,2,1,0:T(8,128)(2,1)} %collective-permute-done.37), channel_id=1, source_target_pairs={{0,31},{1,0},{2,1},{3,2},{4,3},{5,4},{6,5},{7,6},{8,7},{9,8},{10,9... | collective-permute-start | bytes 2359304 | tf_op jit(solution)/shard_map/ppermute | solution.py:12
  672.1 24.0 %copy-start.13 = (bf16[2,8,8,16,6,1]{3,2,4,5,1,0:T(8,128)(2,1)S(1)}, bf16[2,8,8,16,6,1]{3,2,4,5,1,0:T(8,128)(2,1)}, u32[]{:S(2)}) copy-start(bf16[2,8,8,16,6,1]{3,2,4,5,1,0:T(8,128)(2,1)} %copy.58) | copy-start | bytes 73732
where the time goes:
time: 709 us; the launch traced here: 706 us
  starting transfers between devices  462 us (65%)
  waiting for transfers between devices  158 us (22%)
  matrix products  42.3 us (6%)
  local copies, waits for them, and re-layouts  39.6 us (6%)
    ppermute x46, starting transfers between devices, shifted(): return lax.ppermute(value, axis, pairs)  462 us
    ppermute x46, waiting for transfers between devices, shifted(): return lax.ppermute(value, axis, pairs)  158 us
    dot_general x8, matrix products, one_tick(): jnp.einsum('iaokb,kbyz->iaoyz', select, right, preferred_element_type=jnp...  33.1 us
    dot_general x8, local copies, waits for them, and re-layouts, one_tick(): jnp.einsum('iaokb,kbyz->iaoyz', select, right, preferred_element_type=jnp...  26.5 us
  transfers between devices with their start and end apart: 46, of which 20 were waited for; matrix products, arithmetic and copies ran while one was open for 12% of the time, Pallas kernels for 0%

commit v1 on v0

v1 whole, which is shorter than its diff:
```python
import functools

import jax
import jax.numpy as jnp
from jax import lax
from jax.experimental import pallas as pl
from jax.experimental.pallas import tpu as pltpu
from jax.sharding import PartitionSpec as P

TICKS = 8
NEAR = TICKS - 1
MESH = pl.DeviceIdType.MESH


def kernel(
    n_row, n_col, left_hbm, left_cols, right_hbm, right_cols, out_cols, out_ref,
    lraw, rraw, lbuf, dense, wide, part, acc, lcol, ocol,
    local_sem, lc_send, lc_recv, oc_send, oc_recv, far_send, far_recv, y_send, y_recv, sib_send, sib_recv, sum_send, sum_recv,
):
    row = lax.axis_index("row")
    col = lax.axis_index("col")
    y = lax.rem(row // 2, 4)
    half = row // 8
    core = lax.rem(row, 2)
    far = lax.rem(row + 8, n_row)
    sibling = row + 1 - 2 * core
    ib, nl, bs, _ = lraw.shape
    kb = rraw.shape[0]
    nr = rraw.shape[1] - 1
    no = ocol.shape[2]

    get_left = pltpu.make_async_copy(left_hbm, lraw, local_sem.at[0])
    get_right = pltpu.make_async_copy(right_hbm, rraw.at[:, pl.ds(0, nr)], local_sem.at[1])
    get_left.start()
    get_right.start()

    barrier = pltpu.get_barrier_semaphore()
    for d in range(1, n_row):
        pl.semaphore_signal(barrier, inc=1, device_id={"row": lax.rem(row + d, n_row)}, device_id_type=MESH)
    for d in range(1, TICKS):
        for e in (d, n_col - d):
            pl.semaphore_signal(barrier, inc=1, device_id={"col": lax.rem(col + e, n_col)}, device_id_type=MESH)

    def remote(src, dst, send, recv, to):
        return pltpu.make_async_remote_copy(
            src_ref=src, dst_ref=dst, send_sem=send, recv_sem=recv, device_id=to, device_id_type=MESH
        )

    get_left.wait()
    for b in range(ib):
        for a in range(0, nl, 2):
            lbuf[0, b * bs : (b + 1) * bs, a * bs : (a + 2) * bs] = jnp.concatenate(
                [lraw[b, a], lraw[b, a + 1]], axis=1
            )
    for b in range(ib):
        for a in range(nl):
            lcol[0, b, a] = left_cols[b, a]
    for i in range(kb):
        rraw[i, nr] = jnp.zeros((bs, bs), rraw.dtype)

    pl.semaphore_wait(barrier, n_row - 1 + 2 * NEAR)

    def send_ocol(s):
        return remote(out_cols, ocol.at[s], oc_send.at[s], oc_recv.at[s], {"col": lax.rem(col + n_col - NEAR + s, n_col)})

    def send_lcol(s):
        return remote(left_cols, lcol.at[s], lc_send.at[s], lc_recv.at[s], {"row": lax.rem(row + s, n_row)})

    to_far = remote(lbuf.at[0], lbuf.at[TICKS], far_send, far_recv, {"row": far})

    def to_y(d, src):
        return remote(
            lbuf.at[src], lbuf.at[2 * d], y_send.at[d - 1], y_recv.at[d - 1],
            {"row": half * 8 + lax.rem(y + d, 4) * 2 + core},
        )

    def to_sibling(i, src, dst):
        return remote(lbuf.at[src], lbuf.at[dst], sib_send.at[i], sib_recv.at[i], {"row": sibling})

    send_ocol(0).start()
    to_far.start()
    for d in range(1, 4):
        @pl.when(y + d < 4)
        def _():
            to_y(d, 0).start()

    @pl.when(core == 0)
    def _():
        to_sibling(0, 0, 1).start()

    for s in range(1, TICKS):
        if s < NEAR:
            send_ocol(s).start()
        send_lcol(s).start()
    for b in range(ib):
        for o in range(no):
            ocol[NEAR, b, o] = out_cols[b, o]

    get_right.wait()

    def fill(k, carry):
        cols = [right_cols[k, e] for e in range(nr)]

        def slot_of(j):
            slot = jnp.int32(nr)
            for e in range(nr):
                slot = jnp.where(cols[e] == j, e, slot)
            return slot

        for j in range(0, 16, 2):
            dense[k, :, j * bs : (j + 2) * bs] = jnp.concatenate(
                [rraw[k, slot_of(j)], rraw[k, slot_of(j + 1)]], axis=1
            )
        return carry

    lax.fori_loop(0, kb, fill, 0)

    low = lax.broadcasted_iota(jnp.int32, (bs, 2 * bs), 1) < bs

    def product(s):
        for b in range(ib):
            total = None
            for a in range(0, nl, 4):
                rows = jnp.concatenate([dense[lcol[s, b, a + i]] for i in range(4)], axis=0)
                term = jnp.dot(
                    lbuf[s, b * bs : (b + 1) * bs, a * bs : (a + 4) * bs], rows, preferred_element_type=jnp.float32
                )
                total = term if total is None else total + term
            for j in range(8):
                wide[b, j] = total[:, j * 2 * bs : (j + 1) * 2 * bs]
            for o in range(0, no, 2):
                j0 = ocol[s, b, o]
                j1 = ocol[s, b, o + 1]
                v0 = wide[b, j0 // 2]
                v1 = wide[b, j1 // 2]
                w0 = jnp.where(lax.rem(j0, 2) == 1, pltpu.roll(v0, bs, 1), v0)
                w1 = jnp.where(lax.rem(j1, 2) == 1, v1, pltpu.roll(v1, bs, 1))
                part[s, b * bs : (b + 1) * bs, o * bs : (o + 2) * bs] = jnp.where(low, w0, w1)

    def send_sum(s):
        return remote(
            part.at[s], acc.at[s], sum_send.at[s], sum_recv.at[s], {"col": lax.rem(col + 1, n_col)}
        )

    send_ocol(0).wait_recv()
    product(0)
    send_sum(0).start()

    to_far.wait_recv()
    for d in range(1, 4):
        @pl.when(y + d >= 4)
        def _():
            to_y(d, TICKS).start()

    @pl.when(core == 1)
    def _():
        to_sibling(3, TICKS, NEAR).start()

    for d in range(1, 4):
        to_y(d, 0).wait_recv()
        to_sibling(d - core, 2 * d, 2 * (d - core) + 1).start()

    def tick(s, carry):
        @pl.when(lax.rem(s, 2) == 1)
        def _():
            to_sibling(s // 2, 0, s).wait_recv()

        send_lcol(s).wait_recv()

        @pl.when(s < NEAR)
        def _():
            send_ocol(s).wait_recv()

        product(s)
        send_sum(s - 1).wait_recv()
        part[s] = part[s] + acc[s - 1]

        @pl.when(s < NEAR)
        def _():
            send_sum(s).start()

        return carry

    lax.fori_loop(1, TICKS, tick, 0)

    for b in range(ib):
        for o in range(no):
            out_ref[b, o] = part[NEAR, b * bs : (b + 1) * bs, o * bs : (o + 1) * bs]

    to_far.wait_send()
    for d in range(1, 4):
        to_y(d, 0).wait_send()
    for i in range(4):
        to_sibling(i, 0, 1).wait_send()
    for s in range(NEAR):
        send_ocol(s).wait_send()
        send_lcol(s + 1).wait_send()
        send_sum(s).wait_send()


def solution(mesh):
    n_row, n_col = mesh.shape["row"], mesh.shape["col"]

    def on_device(left_blocks, left_cols, right_blocks, right_cols, out_cols):
        left, right = left_blocks[0, 0], right_blocks[0, 0]
        left_cols, right_cols, out_cols = left_cols[0, 0], right_cols[0, 0], out_cols[0, 0]
        ib, nl, bs, _ = left.shape
        kb, nr = right_cols.shape
        no = out_cols.shape[1]
        dma = pltpu.SemaphoreType.DMA
        product = pl.pallas_call(
            functools.partial(kernel, n_row, n_col),
            out_shape=jax.ShapeDtypeStruct((ib, no, bs, bs), jnp.float32),
            in_specs=[
                pl.BlockSpec(memory_space=pl.ANY),
                pl.BlockSpec(memory_space=pltpu.SMEM),
                pl.BlockSpec(memory_space=pl.ANY),
                pl.BlockSpec(memory_space=pltpu.SMEM),
                pl.BlockSpec(memory_space=pltpu.SMEM),
            ],
            out_specs=pl.BlockSpec(memory_space=pltpu.VMEM),
            scratch_shapes=[
                pltpu.VMEM(left.shape, left.dtype),
                pltpu.VMEM((kb, nr + 1, bs, bs), right.dtype),
                pltpu.VMEM((TICKS + 1, ib * bs, nl * bs), left.dtype),
                pltpu.VMEM((kb, bs, 16 * bs), right.dtype),
                pltpu.VMEM((ib, 8, bs, 2 * bs), jnp.float32),
                pltpu.VMEM((TICKS, ib * bs, no * bs), jnp.float32),
                pltpu.VMEM((NEAR, ib * bs, no * bs), jnp.float32),
                pltpu.SMEM((TICKS, ib, nl), jnp.int32),
                pltpu.SMEM((TICKS, ib, no), jnp.int32),
                dma((2,)),
                dma((TICKS,)), dma((TICKS,)),
                dma((TICKS,)), dma((TICKS,)),
                dma, dma,
                dma((3,)), dma((3,)),
                dma((4,)), dma((4,)),
                dma((NEAR,)), dma((NEAR,)),
            ],
            compiler_params=pltpu.CompilerParams(collective_id=0, has_side_effects=True),
        )(left, left_cols, right, right_cols, out_cols)
        return product[None, None]

    blocks = P("row", "col", None, None, None, None)
    table = P("row", "col", None, None)
    return jax.shard_map(
        on_device,
        mesh=mesh,
        in_specs=(blocks, table, blocks, table, table),
        out_specs=blocks,
        check_vma=False,
    )
```

time: 709 us -> 91.6 us (0.13)
  the two profiles are of different devices: /device:TPU:24 before, /device:TPU:32 now
where the time goes in v1:
time: 91.6 us; the launch traced here: 91.4 us
  Pallas kernels  88.1 us (96%)
  local copies, waits for them, and re-layouts  3.24 us (4%)
    pallas_call x1, Pallas kernels, on_device(): pl.pallas_call(functools.partial(kernel, n_row, n_col), out_shape=jax.Sha...  88.1 us
    unnamed x1, local copies, waits for them, and re-layouts  1.89 us

profile of v1, /device:TPU:32, one launch (start us, length us, event | category | flops | bytes accessed | tf_op | source)
XLA Modules:
  0.0 91.4 jit_solution(14480430158221617340)
XLA Ops:
  0.0 1.4 %copy.7 = s32[1,1,16,6]{3,2,1,0:T(8,128)} copy(s32[1,1,16,6]{2,1,3,0:T(1,128)} %param.8) | data formatting | bytes 768 | tf_op jit(solution)/shard_map/squeeze | solution.py:206
  1.4 88.1 %shard_map.55 = f32[2,8,64,64]{3,2,1,0:T(8,128)} custom-call(bf16[2,8,64,64]{3,2,1,0:T(8,128)(2,1)} %bitcast.8, s32[2,8]{1,0:T(2,128)} %bitcast.10, bf16[16,6,64,64]{3,2,1,0:T(8,128)(2,1)} %bitcast.7, s32[16,6]{1,0:T(8,128)} %bitcast.9, s32[2,8]{1,0:T(2,128)} %bitcast.11), custom_call_target="tpu_custom_call" | custom-call | tf_op jit(solution)/shard_map/pallas_call | solution.py:211
  89.5 1.9 %copy.9 = f32[1,1,2,8,64,64]{5,4,3,2,1,0:T(8,128)} copy(f32[1,1,2,8,64,64]{5,4,3,2,1,0:T(8,128)} %bitcast.6) | data formatting | bytes 524288

commit v2 on v1

v2 whole, which is shorter than its diff:
```python
import functools

import jax
import jax.numpy as jnp
from jax import lax
from jax.experimental import pallas as pl
from jax.experimental.pallas import tpu as pltpu
from jax.sharding import PartitionSpec as P

TICKS = 8
NEAR = TICKS - 1
LINE = 8
FULL = 32767.0
MESH = pl.DeviceIdType.MESH


def kernel(
    n_row, n_col, left_hbm, left_cols, right_hbm, right_cols, out_cols, out_ref,
    lraw, rraw, lbuf, dense, wide, part, sent, sent_scale, got, got_scale, lcol, ocol,
    local_sem, lc_send, lc_recv, oc_send, oc_recv, far_send, far_recv, y_send, y_recv, sib_send, sib_recv,
    sum_send, sum_recv, scale_send, scale_recv,
):
    row = lax.axis_index("row")
    col = lax.axis_index("col")
    y = lax.rem(row // 2, 4)
    half = row // 8
    core = lax.rem(row, 2)
    z = lax.rem(col, LINE)
    far = lax.rem(row + 8, n_row)
    sibling = row + 1 - 2 * core
    ib, nl, bs, _ = lraw.shape
    kb = rraw.shape[0]
    nr = rraw.shape[1] - 1
    no = ocol.shape[2]

    get_left = pltpu.make_async_copy(left_hbm, lraw, local_sem.at[0])
    get_right = pltpu.make_async_copy(right_hbm, rraw.at[:, pl.ds(0, nr)], local_sem.at[1])
    get_left.start()
    get_right.start()

    barrier = pltpu.get_barrier_semaphore()
    for d in range(1, n_row):
        pl.semaphore_signal(barrier, inc=1, device_id={"row": lax.rem(row + d, n_row)}, device_id_type=MESH)
    for d in range(1, TICKS):
        for e in (d, n_col - d):
            pl.semaphore_signal(barrier, inc=1, device_id={"col": lax.rem(col + e, n_col)}, device_id_type=MESH)

    def remote(src, dst, send, recv, to):
        return pltpu.make_async_remote_copy(
            src_ref=src, dst_ref=dst, send_sem=send, recv_sem=recv, device_id=to, device_id_type=MESH
        )

    get_left.wait()
    for b in range(ib):
        for a in range(0, nl, 2):
            lbuf[0, b, :, a * bs : (a + 2) * bs] = jnp.concatenate([lraw[b, a], lraw[b, a + 1]], axis=1)
    for b in range(ib):
        for a in range(nl):
            lcol[0, b, a] = left_cols[b, a]
        for o in range(no):
            ocol[NEAR, b, o] = out_cols[b, o]
    for i in range(kb):
        rraw[i, nr] = jnp.zeros((bs, bs), rraw.dtype)

    pl.semaphore_wait(barrier, n_row - 1 + 2 * NEAR)

    def send_ocol(s):
        return remote(out_cols, ocol.at[s], oc_send.at[s], oc_recv.at[s], {"col": lax.rem(col + n_col - NEAR + s, n_col)})

    def send_lcol(s):
        return remote(left_cols, lcol.at[s], lc_send.at[s], lc_recv.at[s], {"row": lax.rem(row + s, n_row)})

    def to_far(b):
        return remote(lbuf.at[0, b], lbuf.at[TICKS, b], far_send.at[b], far_recv.at[b], {"row": far})

    def to_y(d, src, b):
        return remote(
            lbuf.at[src, b], lbuf.at[2 * d, b], y_send.at[d - 1, b], y_recv.at[d - 1, b],
            {"row": half * 8 + lax.rem(y + d, 4) * 2 + core},
        )

    def to_sibling(i, src, dst, b):
        return remote(lbuf.at[src, b], lbuf.at[dst, b], sib_send.at[i, b], sib_recv.at[i, b], {"row": sibling})

    @pl.when(half == 1)
    def _():
        for b in range(ib):
            to_far(b).start()

    for d in range(1, 4):
        @pl.when(y + d < 4)
        def _():
            for b in range(ib):
                to_y(d, 0, b).start()

    @pl.when(core == 0)
    def _():
        for b in range(ib):
            to_sibling(0, 0, 1, b).start()

    for s in range(TICKS):
        if s < NEAR:
            send_ocol(s).start()
        if s > 0:
            send_lcol(s).start()

    get_right.wait()

    def fill(k, carry):
        cols = [right_cols[e, k] for e in range(nr)]

        def slot_of(j):
            slot = jnp.int32(nr)
            for e in range(nr):
                slot = jnp.where(cols[e] == j, e, slot)
            return slot

        for j in range(0, 16, 2):
            dense[k, :, j * bs : (j + 2) * bs] = jnp.concatenate(
                [rraw[k, slot_of(j)], rraw[k, slot_of(j + 1)]], axis=1
            )
        return carry

    lax.fori_loop(0, kb, fill, 0)

    for b in range(ib):
        to_far(b).wait_recv()

        @pl.when(half == 0)
        def _():
            to_far(b).start()

        for d in range(1, 4):
            @pl.when(y + d >= 4)
            def _():
                to_y(d, TICKS, b).start()

        @pl.when(core == 1)
        def _():
            to_sibling(3, TICKS, NEAR, b).start()

    for b in range(ib):
        for d in range(1, 4):
            to_y(d, 0, b).wait_recv()
            to_sibling(d - core, 2 * d, 2 * (d - core) + 1, b).start()

    low = lax.broadcasted_iota(jnp.int32, (bs, 2 * bs), 1) < bs

    def product(s):
        send_lcol_wait = s > 0

        @pl.when(send_lcol_wait)
        def _():
            send_lcol(s).wait_recv()

        @pl.when(s < NEAR)
        def _():
            send_ocol(s).wait_recv()

        for b in range(ib):
            @pl.when(lax.rem(s, 2) == 1)
            def _():
                to_sibling(s // 2, 0, s, b).wait_recv()

            total = None
            for a in range(0, nl, 4):
                rows = jnp.concatenate([dense[lcol[s, b, a + i]] for i in range(4)], axis=0)
                term = jnp.dot(lbuf[s, b, :, a * bs : (a + 4) * bs], rows, preferred_element_type=jnp.float32)
                total = term if total is None else total + term
            for j in range(8):
                wide[b, j] = total[:, j * 2 * bs : (j + 1) * 2 * bs]
            for o in range(0, no, 2):
                j0 = ocol[s, b, o]
                j1 = ocol[s, b, o + 1]
                v0 = wide[b, j0 // 2]
                v1 = wide[b, j1 // 2]
                w0 = jnp.where(lax.rem(j0, 2) == 1, pltpu.roll(v0, bs, 1), v0)
                w1 = jnp.where(lax.rem(j1, 2) == 1, v1, pltpu.roll(v1, bs, 1))
                part[s, b, :, o * bs : (o + 2) * bs] = jnp.where(low, w0, w1)

    def send_sum(s, slot, to, b):
        to = {"col": lax.rem(to, n_col)}
        return (
            remote(sent.at[s, b], got.at[slot, b], sum_send.at[s, b], sum_recv.at[slot, b], to),
            remote(sent_scale.at[s, b], got_scale.at[slot, b], scale_send.at[s, b], scale_recv.at[slot, b], to),
        )

    def receive(s, slot, b):
        for copy in send_sum(0, slot, col + 1, b):
            copy.wait_recv()
        part[s, b] = part[s, b] + got[slot, b].astype(jnp.float32) * got_scale[slot, b]

    def pass_on(s, slot, to, has_input):
        for b in range(ib):
            @pl.when(has_input)
            def _():
                receive(s, s, b)

            total = part[s, b]
            top = jnp.maximum(jnp.max(jnp.abs(total), axis=0, keepdims=True), 1e-30)
            sent[s, b] = jnp.round(total * (FULL / top)).astype(jnp.int32).astype(jnp.int16)
            sent_scale[s, b] = top * (1.0 / FULL)
            for copy in send_sum(s, slot, to, b):
                copy.start()

    def products(t):
        @pl.when(t >= z)
        def _():
            product(t)

        @pl.when((t >= LINE - 1 - z) & (t < NEAR))
        def _():
            product(NEAR - 1 - t)

    def step(t, carry):
        @pl.when(t >= z)
        def _():
            pass_on(t, t + 1, col + 1, z > 0)

        @pl.when(t >= LINE - 1 - z)
        def _():
            s = NEAR - 1 - t
            first = s == 0
            pass_on(
                s, jnp.where(first, TICKS, s - 1), jnp.where(first, col + LINE - 1, col + n_col - 1), z < LINE - 1
            )

        products(t + 1)
        return carry

    products(jnp.int32(0))
    lax.fori_loop(0, NEAR, step, 0)

    for b in range(ib):
        @pl.when(z > 0)
        def _():
            receive(NEAR, NEAR, b)

        @pl.when(z < LINE - 1)
        def _():
            receive(NEAR, TICKS, b)

        for o in range(no):
            out_ref[b, o] = part[NEAR, b, :, o * bs : (o + 1) * bs]

    for b in range(ib):
        to_far(b).wait_send()
        for d in range(1, 4):
            to_y(d, 0, b).wait_send()
        for i in range(4):
            to_sibling(i, 0, 1, b).wait_send()
        for s in range(NEAR):
            for copy in send_sum(s, 0, col + 1, b):
                copy.wait_send()
    for s in range(NEAR):
        send_ocol(s).wait_send()
        send_lcol(s + 1).wait_send()


def solution(mesh):
    n_row, n_col = mesh.shape["row"], mesh.shape["col"]

    def on_device(left_blocks, left_cols, right_blocks, right_cols, out_cols):
        left, right = left_blocks[0, 0], right_blocks[0, 0]
        left_cols, right_cols, out_cols = left_cols[0, 0], right_cols[0, 0].T, out_cols[0, 0]
        ib, nl, bs, _ = left.shape
        nr, kb = right_cols.shape
        no = out_cols.shape[1]
        dma = pltpu.SemaphoreType.DMA
        product = pl.pallas_call(
            functools.partial(kernel, n_row, n_col),
            out_shape=jax.ShapeDtypeStruct((ib, no, bs, bs), jnp.float32),
            in_specs=[
                pl.BlockSpec(memory_space=pl.ANY),
                pl.BlockSpec(memory_space=pltpu.SMEM),
                pl.BlockSpec(memory_space=pl.ANY),
                pl.BlockSpec(memory_space=pltpu.SMEM),
                pl.BlockSpec(memory_space=pltpu.SMEM),
            ],
            out_specs=pl.BlockSpec(memory_space=pltpu.VMEM),
            scratch_shapes=[
                pltpu.VMEM(left.shape, left.dtype),
                pltpu.VMEM((kb, nr + 1, bs, bs), right.dtype),
                pltpu.VMEM((TICKS + 1, ib, bs, nl * bs), left.dtype),
                pltpu.VMEM((kb, bs, 16 * bs), right.dtype),
                pltpu.VMEM((ib, 8, bs, 2 * bs), jnp.float32),
                pltpu.VMEM((TICKS, ib, bs, no * bs), jnp.float32),
                pltpu.VMEM((NEAR, ib, bs, no * bs), jnp.int16),
                pltpu.VMEM((NEAR, ib, 1, no * bs), jnp.float32),
                pltpu.VMEM((TICKS + 1, ib, bs, no * bs), jnp.int16),
                pltpu.VMEM((TICKS + 1, ib, 1, no * bs), jnp.float32),
                pltpu.SMEM((TICKS, ib, nl), jnp.int32),
                pltpu.SMEM((TICKS, ib, no), jnp.int32),
                dma((2,)),
                dma((TICKS,)), dma((TICKS,)),
                dma((TICKS,)), dma((TICKS,)),
                dma((ib,)), dma((ib,)),
                dma((3, ib)), dma((3, ib)),
                dma((4, ib)), dma((4, ib)),
                dma((NEAR, ib)), dma((TICKS + 1, ib)),
                dma((NEAR, ib)), dma((TICKS + 1, ib)),
            ],
            compiler_params=pltpu.CompilerParams(collective_id=0, has_side_effects=True),
        )(left, left_cols, right, right_cols, out_cols)
        return product[None, None]

    blocks = P("row", "col", None, None, None, None)
    table = P("row", "col", None, None)
    return jax.shard_map(
        on_device,
        mesh=mesh,
        in_specs=(blocks, table, blocks, table, table),
        out_specs=blocks,
        check_vma=False,
    )
```

time: 91.6 us -> 78 us (0.85)
  the two profiles are of different devices: /device:TPU:32 before, /device:TPU:322 now
where the time goes in v2:
time: 78 us; the launch traced here: 77.8 us
  Pallas kernels  74.6 us (96%)
  local copies, waits for them, and re-layouts  3.16 us (4%)
    pallas_call x1, Pallas kernels, on_device(): pl.pallas_call(functools.partial(kernel, n_row, n_col), out_shape=jax.Sha...  74.6 us
    unnamed x2, local copies, waits for them, and re-layouts  3.16 us

profile of v2, /device:TPU:322, one launch (start us, length us, event | category | flops | bytes accessed | tf_op | source)
XLA Modules:
  0.0 77.8 jit_solution(13841239863203635880)
XLA Ops:
  0.0 1.3 %copy.8 = s32[1,1,16,6]{2,3,1,0:T(8,128)} copy(s32[1,1,16,6]{2,1,3,0:T(1,128)} %param.8) | data formatting | bytes 768
  1.3 74.6 %shard_map.55 = f32[2,8,64,64]{3,2,1,0:T(8,128)} custom-call(bf16[2,8,64,64]{3,2,1,0:T(8,128)(2,1)} %bitcast.12, s32[2,8]{1,0:T(2,128)} %bitcast.14, bf16[16,6,64,64]{3,2,1,0:T(8,128)(2,1)} %bitcast.11, s32[6,16]{1,0:T(8,128)} %bitcast.13, s32[2,8]{1,0:T(2,128)} %bitcast.15), custom_call_target="tpu_custom_call" | custom-call | tf_op jit(solution)/shard_map/pallas_call | solution.py:270
  75.9 1.9 %copy.10 = f32[1,1,2,8,64,64]{5,4,3,2,1,0:T(8,128)} copy(f32[1,1,2,8,64,64]{5,4,3,2,1,0:T(8,128)} %bitcast.10) | data formatting | bytes 524288

commit v3 on v1

v3 whole, which is shorter than its diff:
```python
import functools

import jax
import jax.numpy as jnp
from jax import lax
from jax.experimental import pallas as pl
from jax.experimental.pallas import tpu as pltpu
from jax.sharding import PartitionSpec as P

TICKS = 8
NEAR = TICKS - 1
LINE = 8
FULL = 32767.0
SUB = 2
MESH = pl.DeviceIdType.MESH


def kernel(
    n_row, n_col, left_hbm, left_cols, right_hbm, right_cols, out_cols, out_ref,
    lraw, rraw, lbuf, dense, wide, part, sent, sent_scale, got, got_scale, lcol, ocol,
    local_sem, oc_send, oc_recv, far_send, far_recv, y_send, y_recv, sib_send, sib_recv,
    sum_send, sum_recv, scale_send, scale_recv, far_ready,
):
    row = lax.axis_index("row")
    col = lax.axis_index("col")
    y = lax.rem(row // 2, 4)
    half = row // 8
    core = lax.rem(row, 2)
    z = lax.rem(col, LINE)
    line = col - z
    far = lax.rem(row + 8, n_row)
    sibling = row + 1 - 2 * core
    ib, nl, bs, _ = lraw.shape
    kb = rraw.shape[0]
    nr = rraw.shape[1] - 1
    no = ocol.shape[2]
    sub = bs // SUB

    get_left = pltpu.make_async_copy(left_hbm, lraw, local_sem.at[0])
    get_right = pltpu.make_async_copy(right_hbm, rraw.at[:, pl.ds(0, nr)], local_sem.at[1])
    get_left.start()
    get_right.start()

    barrier = pltpu.get_barrier_semaphore()

    def greet(to):
        pl.semaphore_signal(barrier, inc=1, device_id=to, device_id_type=MESH)

    def y_row(d):
        return half * 8 + lax.rem(y + d, 4) * 2 + core

    def apart(n):
        return line + z + n - 2 * n * lax.rem(z // n, 2)

    @pl.when(half == 0)
    def _():
        greet({"row": far})

    greet({"row": sibling})
    for d in range(1, 4):
        greet({"row": y_row(d)})
    for n in (1, 2, 4):
        greet({"col": apart(n)})
    for d in (LINE, n_col - LINE):
        greet({"col": lax.rem(col + d, n_col)})
    inside = (z > 0) & (z < LINE - 1)

    @pl.when(inside)
    def _():
        greet({"col": line + z - 1 + 2 * lax.rem(z, 2)})

    @pl.when(z > 0)
    def _():
        greet({"col": lax.rem(col + LINE - 1, n_col)})

    @pl.when(z < LINE - 1)
    def _():
        greet({"col": lax.rem(col + n_col - LINE + 1, n_col)})

    def remote(src, dst, send, recv, to):
        return pltpu.make_async_remote_copy(
            src_ref=src, dst_ref=dst, send_sem=send, recv_sem=recv, device_id=to, device_id_type=MESH
        )

    get_left.wait()
    for b in range(ib):
        for a in range(0, nl, 2):
            lbuf[0, b, :, a * bs : (a + 2) * bs] = jnp.concatenate([lraw[b, a], lraw[b, a + 1]], axis=1)
    for b in range(ib):
        for a in range(nl):
            lcol[0, b, a] = left_cols[b, a]
        for o in range(no):
            ocol[z, b, o] = out_cols[b, o]
    for i in range(kb):
        rraw[i, nr] = jnp.zeros((bs, bs), rraw.dtype)

    pl.semaphore_wait(barrier, jnp.where(inside, 12, 10) + half)

    def panel(src, dst, send, recv, to, b):
        copies = [remote(lbuf.at[src, b], lbuf.at[dst, b], send.at[b], recv.at[b], to)]
        if b == 0:
            copies.append(remote(lcol.at[src], lcol.at[dst], send.at[ib], recv.at[ib], to))
        return copies

    def to_far(b):
        return panel(0, TICKS, far_send, far_recv, {"row": far}, b)

    def to_y(d, src, b):
        return panel(src, 2 * d, y_send.at[d - 1], y_recv.at[d - 1], {"row": y_row(d)}, b)

    def to_sibling(i, src, dst, b):
        return panel(src, dst, sib_send.at[i], sib_recv.at[i], {"row": sibling}, b)

    def start(copies):
        for copy in copies:
            copy.start()

    def wait_recv(copies):
        for copy in copies:
            copy.wait_recv()

    def wait_send(copies):
        for copy in copies:
            copy.wait_send()

    def to_apart(i):
        n = 1 << i
        mine = pl.ds(z // n * n, n)
        return remote(ocol.at[mine], ocol.at[mine], oc_send.at[i], oc_recv.at[i], {"col": apart(n)})

    to_line = remote(
        ocol.at[pl.ds(0, LINE)], ocol.at[pl.ds(LINE, LINE)], oc_send.at[3], oc_recv.at[3],
        {"col": lax.rem(col + n_col - LINE, n_col)},
    )

    @pl.when(half == 1)
    def _():
        pl.semaphore_signal(far_ready, inc=1, device_id={"row": far}, device_id_type=MESH)
        start(to_far(0))

    to_apart(0).start()
    for b in range(ib):
        for d in range(1, 4):
            @pl.when(y + d < 4)
            def _():
                start(to_y(d, 0, b))

    @pl.when(core == 0)
    def _():
        for b in range(ib):
            start(to_sibling(0, 0, 1, b))

    get_right.wait()

    def fill(k, carry):
        cols = [right_cols[0, e, 0, k] for e in range(nr)]

        def slot_of(j):
            slot = jnp.int32(nr)
            for e in range(nr):
                slot = jnp.where(cols[e] == j, e, slot)
            return slot

        for j in range(0, 16, 2):
            dense[k, :, j * bs : (j + 2) * bs] = jnp.concatenate(
                [rraw[k, slot_of(j)], rraw[k, slot_of(j + 1)]], axis=1
            )
        return carry

    lax.fori_loop(0, kb // 2, fill, 0)

    @pl.when(half == 1)
    def _():
        start(to_far(1))

    to_apart(0).wait_recv()
    to_apart(1).start()
    lax.fori_loop(kb // 2, kb, fill, 0)
    to_apart(1).wait_recv()
    to_apart(2).start()
    to_apart(2).wait_recv()
    to_line.start()

    low = lax.broadcasted_iota(jnp.int32, (bs, 2 * bs), 1) < bs

    def product(s, b, u):
        target = z + NEAR - s
        total = None
        for a in range(0, nl, 4):
            rows = jnp.concatenate([dense[lcol[s, b, a + n]] for n in range(4)], axis=0)
            term = jnp.dot(lbuf[s, b, :, a * bs : (a + 4) * bs], rows, preferred_element_type=jnp.float32)
            total = term if total is None else total + term
        for j in range(8):
            wide[u, j] = total[:, j * 2 * bs : (j + 1) * 2 * bs]
        for o in range(0, no, 2):
            j0 = ocol[target, b, o]
            j1 = ocol[target, b, o + 1]
            v0 = wide[u, j0 // 2]
            v1 = wide[u, j1 // 2]
            w0 = jnp.where(lax.rem(j0, 2) == 1, pltpu.roll(v0, bs, 1), v0)
            w1 = jnp.where(lax.rem(j1, 2) == 1, v1, pltpu.roll(v1, bs, 1))
            both = jnp.where(low, w0, w1)
            for h in range(SUB):
                part[s, b * SUB + h, :, o * bs : (o + 2) * bs] = both[h * sub : (h + 1) * sub]

    def send_sum(s, slot, to, g):
        to = {"col": lax.rem(to, n_col)}
        return (
            remote(sent.at[s, g], got.at[slot, g], sum_send.at[s, g], sum_recv.at[slot, g], to),
            remote(sent_scale.at[s, g], got_scale.at[slot, g], scale_send.at[s, g], scale_recv.at[slot, g], to),
        )

    def receive(s, slot, g):
        wait_recv(send_sum(0, slot, col + 1, g))
        part[s, g] = part[s, g] + got[slot, g].astype(jnp.float32) * got_scale[slot, g]

    def pass_on(s, slot, to, has_input, g):
        @pl.when(has_input)
        def _():
            receive(s, s, g)

        total = part[s, g]
        top = jnp.maximum(jnp.max(jnp.abs(total), axis=0, keepdims=True), 1e-30)
        sent[s, g] = jnp.round(total * (FULL / top)).astype(jnp.int32).astype(jnp.int16)
        sent_scale[s, g] = top * (1.0 / FULL)
        start(send_sum(s, slot, to, g))

    def step(t, b):
        chunks = range(b * SUB, (b + 1) * SUB)

        @pl.when((t >= z) & (t > 0))
        def _():
            for g in chunks:
                pass_on(t, t + 1, col + 1, z > 0, g)

        @pl.when((t >= LINE - 1 - z) & ((t < NEAR - 1) | (z < LINE - 1)))
        def _():
            s = NEAR - 1 - t
            first = s == 0
            slot = jnp.where(first, TICKS, s - 1)
            to = jnp.where(first, col + LINE - 1, col + n_col - 1)
            for g in chunks:
                pass_on(s, slot, to, z < LINE - 1, g)

    def products(i, b):
        if i < 4:
            product(i, b, 0)
            product(NEAR - i, b, 1)
        else:
            product(NEAR, b, 0)

    def from_far(b):
        wait_recv(to_far(b))
        for d in range(1, 4):
            @pl.when(y + d >= 4)
            def _():
                start(to_y(d, TICKS, b))

        @pl.when(core == 1)
        def _():
            start(to_sibling(3, TICKS, NEAR, b))

    def collect(b):
        for d in range(1, 4):
            wait_recv(to_y(d, 0, b))
            start(to_sibling(d - core, 2 * d, 2 * (d - core) + 1, b))

    def from_sibling(b):
        for i in range(4):
            wait_recv(to_sibling(i, 0, 1, b))

    to_line.wait_recv()
    for b in range(ib):
        product(0, b, b)

    @pl.when(z == 0)
    def _():
        for g in range(ib * SUB):
            pass_on(0, 1, col + 1, z > 0, g)

    @pl.when(z == LINE - 1)
    def _():
        for g in range(ib * SUB):
            pass_on(0, TICKS, col + LINE - 1, z < LINE - 1, g)

    @pl.when(half == 0)
    def _():
        pl.semaphore_wait(far_ready, 1)
        start(to_far(0))

    from_far(0)
    collect(0)

    @pl.when(half == 0)
    def _():
        start(to_far(1))

    from_far(1)
    from_sibling(0)
    products(1, 0)
    step(jnp.int32(0), 0)
    products(2, 0)
    step(jnp.int32(1), 0)
    collect(1)
    products(3, 0)
    products(4, 0)
    from_sibling(1)
    products(1, 1)
    step(jnp.int32(0), 1)
    products(2, 1)
    step(jnp.int32(1), 1)
    products(3, 1)
    products(4, 1)

    def steps(t, carry):
        for b in range(ib):
            step(t, b)
        return carry

    lax.fori_loop(2, NEAR, steps, 0)

    for g in range(ib * SUB):
        @pl.when(z > 0)
        def _():
            receive(NEAR, NEAR, g)

        @pl.when(z < LINE - 1)
        def _():
            receive(NEAR, TICKS, g)

        for o in range(no):
            out_ref[g // SUB, o, g % SUB * sub : (g % SUB + 1) * sub] = part[NEAR, g, :, o * bs : (o + 1) * bs]

    for b in range(ib):
        wait_send(to_far(b))
        for d in range(1, 4):
            wait_send(to_y(d, 0, b))
        for i in range(4):
            wait_send(to_sibling(i, 0, 1, b))
    for s in range(NEAR):
        for g in range(ib * SUB):
            wait_send(send_sum(s, 0, col + 1, g))
    for i in range(3):
        to_apart(i).wait_send()
    to_line.wait_send()


def solution(mesh):
    n_row, n_col = mesh.shape["row"], mesh.shape["col"]

    def on_device(left_blocks, left_cols, right_blocks, right_cols, out_cols):
        left, right = left_blocks[0, 0], right_blocks[0, 0]
        left_cols, right_cols, out_cols = left_cols[0, 0], lax.transpose(right_cols, (0, 3, 1, 2)), out_cols[0, 0]
        ib, nl, bs, _ = left.shape
        _, nr, _, kb = right_cols.shape
        no = out_cols.shape[1]
        dma = pltpu.SemaphoreType.DMA
        product = pl.pallas_call(
            functools.partial(kernel, n_row, n_col),
            out_shape=jax.ShapeDtypeStruct((ib, no, bs, bs), jnp.float32),
            in_specs=[
                pl.BlockSpec(memory_space=pl.ANY),
                pl.BlockSpec(memory_space=pltpu.SMEM),
                pl.BlockSpec(memory_space=pl.ANY),
                pl.BlockSpec(memory_space=pltpu.SMEM),
                pl.BlockSpec(memory_space=pltpu.SMEM),
            ],
            out_specs=pl.BlockSpec(memory_space=pltpu.VMEM),
            scratch_shapes=[
                pltpu.VMEM(left.shape, left.dtype),
                pltpu.VMEM((kb, nr + 1, bs, bs), right.dtype),
                pltpu.VMEM((TICKS + 1, ib, bs, nl * bs), left.dtype),
                pltpu.VMEM((kb, bs, 16 * bs), right.dtype),
                pltpu.VMEM((ib, 8, bs, 2 * bs), jnp.float32),
                pltpu.VMEM((TICKS, ib * SUB, bs // SUB, no * bs), jnp.float32),
                pltpu.VMEM((NEAR, ib * SUB, bs // SUB, no * bs), jnp.int16),
                pltpu.VMEM((NEAR, ib * SUB, 1, no * bs), jnp.float32),
                pltpu.VMEM((TICKS + 1, ib * SUB, bs // SUB, no * bs), jnp.int16),
                pltpu.VMEM((TICKS + 1, ib * SUB, 1, no * bs), jnp.float32),
                pltpu.SMEM((TICKS + 1, ib, nl), jnp.int32),
                pltpu.SMEM((2 * LINE, ib, no), jnp.int32),
                dma((2,)),
                dma((4,)), dma((4,)),
                dma((ib + 1,)), dma((ib + 1,)),
                dma((3, ib + 1)), dma((3, ib + 1)),
                dma((4, ib + 1)), dma((4, ib + 1)),
                dma((NEAR, ib * SUB)), dma((TICKS + 1, ib * SUB)),
                dma((NEAR, ib * SUB)), dma((TICKS + 1, ib * SUB)),
                pltpu.SemaphoreType.REGULAR,
            ],
            compiler_params=pltpu.CompilerParams(collective_id=0, has_side_effects=True),
        )(left, left_cols, right, right_cols, out_cols)
        return product[None, None]

    blocks = P("row", "col", None, None, None, None)
    table = P("row", "col", None, None)
    return jax.shard_map(
        on_device,
        mesh=mesh,
        in_specs=(blocks, table, blocks, table, table),
        out_specs=blocks,
        check_vma=False,
    )
```

time: 91.6 us -> 70 us (0.76)
  the two profiles are of different devices: /device:TPU:32 before, /device:TPU:288 now
where the time goes in v3:
time: 70 us; the launch traced here: 69.8 us
  Pallas kernels  67.9 us (97%)
  local copies, waits for them, and re-layouts  1.89 us (3%)
    pallas_call x1, Pallas kernels, on_device(): pl.pallas_call(functools.partial(kernel, n_row, n_col), out_shape=jax.Sha...  67.9 us
    unnamed x1, local copies, waits for them, and re-layouts  1.89 us

profile of v3, /device:TPU:288, one launch (start us, length us, event | category | flops | bytes accessed | tf_op | source)
XLA Modules:
  0.0 69.8 jit_solution(9796317582039157016)
XLA Ops:
  0.0 67.9 %shard_map.55 = f32[2,8,64,64]{3,2,1,0:T(8,128)} custom-call(bf16[2,8,64,64]{3,2,1,0:T(8,128)(2,1)} %bitcast.8, s32[2,8]{1,0:T(2,128)} %bitcast.10, bf16[16,6,64,64]{3,2,1,0:T(8,128)(2,1)} %bitcast.7, s32[1,6,1,16]{3,2,1,0:T(1,128)} %bitcast.9, s32[2,8]{1,0:T(2,128)} %bitcast.11), custom_call_target="tpu_custom_call" | custom-call | tf_op jit(solution)/shard_map/pallas_call | solution.py:358
  67.9 1.9 %copy.7 = f32[1,1,2,8,64,64]{5,4,3,2,1,0:T(8,128)} copy(f32[1,1,2,8,64,64]{5,4,3,2,1,0:T(8,128)} %bitcast.6) | data formatting | bytes 524288

commit v4 on v3

--- a/solution.py
+++ b/solution.py
@@ -10,6 +10,7 @@
 TICKS = 8
 NEAR = TICKS - 1
 LINE = 8
+QUAD = 4
 FULL = 32767.0
 SUB = 2
 MESH = pl.DeviceIdType.MESH
@@ -28,6 +29,8 @@
     core = lax.rem(row, 2)
     z = lax.rem(col, LINE)
     line = col - z
+    upper = z // QUAD
+    place = lax.rem(z, QUAD)
     far = lax.rem(row + 8, n_row)
     sibling = row + 1 - 2 * core
     ib, nl, bs, _ = lraw.shape
@@ -49,9 +52,6 @@
     def y_row(d):
         return half * 8 + lax.rem(y + d, 4) * 2 + core
 
-    def apart(n):
-        return line + z + n - 2 * n * lax.rem(z // n, 2)
-
     @pl.when(half == 0)
     def _():
         greet({"row": far})
@@ -59,23 +59,26 @@
     greet({"row": sibling})
     for d in range(1, 4):
         greet({"row": y_row(d)})
-    for n in (1, 2, 4):
-        greet({"col": apart(n)})
-    for d in (LINE, n_col - LINE):
-        greet({"col": lax.rem(col + d, n_col)})
-    inside = (z > 0) & (z < LINE - 1)
-
-    @pl.when(inside)
-    def _():
-        greet({"col": line + z - 1 + 2 * lax.rem(z, 2)})
-
-    @pl.when(z > 0)
-    def _():
-        greet({"col": lax.rem(col + LINE - 1, n_col)})
-
-    @pl.when(z < LINE - 1)
+    for i in range(1, QUAD):
+        greet({"col": line + QUAD * upper + lax.rem(place + i, QUAD)})
+    ahead = lax.rem(col + LINE, n_col)
+    greet({"col": ahead})
+
+    greet({"col": jnp.where(upper == 1, ahead - QUAD, col + QUAD)})
+
+    @pl.when(place < QUAD - 1)
     def _():
         greet({"col": lax.rem(col + n_col - LINE + 1, n_col)})
+
+    @pl.when(upper == 1)
+    def _():
+        greet({"col": line + QUAD - 1})
+
+    @pl.when(upper == 0)
+    def _():
+        greet({"col": lax.rem(col + n_col - QUAD - z, n_col)})
+
+    n_greeted = 9 + half + jnp.where(z == 0, 0, jnp.where(z == QUAD - 1, 5, jnp.where(z == QUAD, 4, 1)))
 
     def remote(src, dst, send, recv, to):
         return pltpu.make_async_remote_copy(
@@ -94,7 +97,7 @@
     for i in range(kb):
         rraw[i, nr] = jnp.zeros((bs, bs), rraw.dtype)
 
-    pl.semaphore_wait(barrier, jnp.where(inside, 12, 10) + half)
+    pl.semaphore_wait(barrier, n_greeted)
 
     def panel(src, dst, send, recv, to, b):
         copies = [remote(lbuf.at[src, b], lbuf.at[dst, b], send.at[b], recv.at[b], to)]
@@ -123,14 +126,24 @@
         for copy in copies:
             copy.wait_send()
 
-    def to_apart(i):
-        n = 1 << i
-        mine = pl.ds(z // n * n, n)
-        return remote(ocol.at[mine], ocol.at[mine], oc_send.at[i], oc_recv.at[i], {"col": apart(n)})
-
-    to_line = remote(
-        ocol.at[pl.ds(0, LINE)], ocol.at[pl.ds(LINE, LINE)], oc_send.at[3], oc_recv.at[3],
-        {"col": lax.rem(col + n_col - LINE, n_col)},
+    def to_mate(i):
+        return remote(
+            out_cols, ocol.at[z], oc_send.at[i - 1], oc_recv.at[i - 1], {"col": line + QUAD * upper + lax.rem(place + i, QUAD)}
+        )
+
+    def from_mate(i):
+        return remote(
+            out_cols, ocol.at[QUAD * upper + lax.rem(place + QUAD - i, QUAD)], oc_send.at[i - 1], oc_recv.at[i - 1],
+            {"col": line + QUAD * upper + lax.rem(place + QUAD - i, QUAD)},
+        )
+
+    quad = pl.ds(QUAD * upper, QUAD)
+    back = pl.ds(LINE + QUAD * upper, QUAD)
+    low_back = pl.ds(jnp.where(upper == 1, QUAD, LINE), QUAD)
+    behind = lax.rem(col + n_col - LINE, n_col)
+    to_behind = remote(ocol.at[quad], ocol.at[back], oc_send.at[3], oc_recv.at[3], {"col": behind})
+    to_other = remote(
+        ocol.at[quad], ocol.at[low_back], oc_send.at[4], oc_recv.at[4], {"col": jnp.where(upper == 1, col - QUAD, behind + QUAD)}
     )
 
     @pl.when(half == 1)
@@ -138,7 +151,8 @@
         pl.semaphore_signal(far_ready, inc=1, device_id={"row": far}, device_id_type=MESH)
         start(to_far(0))
 
-    to_apart(0).start()
+    for i in range(1, QUAD):
+        to_mate(i).start()
     for b in range(ib):
         for d in range(1, 4):
             @pl.when(y + d < 4)
@@ -173,13 +187,17 @@
     def _():
         start(to_far(1))
 
-    to_apart(0).wait_recv()
-    to_apart(1).start()
     lax.fori_loop(kb // 2, kb, fill, 0)
-    to_apart(1).wait_recv()
-    to_apart(2).start()
-    to_apart(2).wait_recv()
-    to_line.start()
+    for i in range(1, QUAD):
+        from_mate(i).wait_recv()
+    to_behind.start()
+    to_other.start()
+
+    @pl.when(half == 0)
+    def _():
+        pl.semaphore_wait(far_ready, 1)
+        for b in range(ib):
+            start(to_far(b))
 
     low = lax.broadcasted_iota(jnp.int32, (bs, 2 * bs), 1) < bs
 
@@ -221,31 +239,48 @@
 
         total = part[s, g]
         top = jnp.maximum(jnp.max(jnp.abs(total), axis=0, keepdims=True), 1e-30)
+        sums, scales = send_sum(s, slot, to, g)
+        sent_scale[s, g] = top * (1.0 / FULL)
+        scales.start()
         sent[s, g] = jnp.round(total * (FULL / top)).astype(jnp.int32).astype(jnp.int16)
-        sent_scale[s, g] = top * (1.0 / FULL)
-        start(send_sum(s, slot, to, g))
+        sums.start()
+
+    def up(s, g):
+        last = z == QUAD - 1
+        pass_on(
+            s, jnp.where(last, TICKS + 1, s + 1), jnp.where(last, col + NEAR - s, col + 1), place > 0, g
+        )
+
+    def down(s, g):
+        across = z == QUAD
+        ends = across | (s == 0)
+        pass_on(
+            s,
+            jnp.where(across, TICKS + 2, jnp.where(ends, TICKS, s - 1)),
+            jnp.where(ends, col + NEAR - s, col + n_col - 1),
+            place < QUAD - 1,
+            g,
+        )
 
     def step(t, b):
         chunks = range(b * SUB, (b + 1) * SUB)
-
-        @pl.when((t >= z) & (t > 0))
+        s_up = t + QUAD * upper
+        s_down = 2 + QUAD * upper - t
+
+        @pl.when((t >= place) & (s_up < NEAR) & (s_up > 0))
         def _():
             for g in chunks:
-                pass_on(t, t + 1, col + 1, z > 0, g)
-
-        @pl.when((t >= LINE - 1 - z) & ((t < NEAR - 1) | (z < LINE - 1)))
-        def _():
-            s = NEAR - 1 - t
-            first = s == 0
-            slot = jnp.where(first, TICKS, s - 1)
-            to = jnp.where(first, col + LINE - 1, col + n_col - 1)
+                up(s_up, g)
+
+        @pl.when((s_down >= 0) & (s_down < z) & ((s_down > 0) | (place < QUAD - 1)))
+        def _():
             for g in chunks:
-                pass_on(s, slot, to, z < LINE - 1, g)
+                down(s_down, g)
 
     def products(i, b):
-        if i < 4:
-            product(i, b, 0)
-            product(NEAR - i, b, 1)
+        if i < 3:
+            product(jnp.where(upper == 1, (4, 5, 2)[i], (1, 3, 5)[i]), b, 0)
+            product(jnp.where(upper == 1, (6, 3, 1)[i], (2, 4, 6)[i]), b, 1)
         else:
             product(NEAR, b, 0)
 
@@ -269,48 +304,39 @@
         for i in range(4):
             wait_recv(to_sibling(i, 0, 1, b))
 
-    to_line.wait_recv()
+    to_behind.wait_recv()
+    to_other.wait_recv()
     for b in range(ib):
         product(0, b, b)
 
     @pl.when(z == 0)
     def _():
         for g in range(ib * SUB):
-            pass_on(0, 1, col + 1, z > 0, g)
-
-    @pl.when(z == LINE - 1)
+            up(0, g)
+
+    @pl.when(place == QUAD - 1)
     def _():
         for g in range(ib * SUB):
-            pass_on(0, TICKS, col + LINE - 1, z < LINE - 1, g)
-
-    @pl.when(half == 0)
-    def _():
-        pl.semaphore_wait(far_ready, 1)
-        start(to_far(0))
+            down(0, g)
 
     from_far(0)
     collect(0)
-
-    @pl.when(half == 0)
-    def _():
-        start(to_far(1))
-
     from_far(1)
     from_sibling(0)
+    products(0, 0)
+    step(jnp.int32(0), 0)
     products(1, 0)
-    step(jnp.int32(0), 0)
-    products(2, 0)
     step(jnp.int32(1), 0)
     collect(1)
+    products(2, 0)
     products(3, 0)
-    products(4, 0)
     from_sibling(1)
+    products(0, 1)
+    step(jnp.int32(0), 1)
     products(1, 1)
-    step(jnp.int32(0), 1)
+    step(jnp.int32(1), 1)
     products(2, 1)
-    step(jnp.int32(1), 1)
     products(3, 1)
-    products(4, 1)
 
     def steps(t, carry):
         for b in range(ib):
@@ -320,13 +346,15 @@
     lax.fori_loop(2, NEAR, steps, 0)
 
     for g in range(ib * SUB):
-        @pl.when(z > 0)
+        @pl.when(place > 0)
         def _():
             receive(NEAR, NEAR, g)
 
-        @pl.when(z < LINE - 1)
+        @pl.when(place < QUAD - 1)
         def _():
             receive(NEAR, TICKS, g)
+
+        receive(NEAR, TICKS + 2 - upper, g)
 
         for o in range(no):
             out_ref[g // SUB, o, g % SUB * sub : (g % SUB + 1) * sub] = part[NEAR, g, :, o * bs : (o + 1) * bs]
@@ -340,9 +368,10 @@
     for s in range(NEAR):
         for g in range(ib * SUB):
             wait_send(send_sum(s, 0, col + 1, g))
-    for i in range(3):
-        to_apart(i).wait_send()
-    to_line.wait_send()
+    for i in range(1, QUAD):
+        to_mate(i).wait_send()
+    to_behind.wait_send()
+    to_other.wait_send()
 
 
 def solution(mesh):
@@ -375,17 +404,17 @@
                 pltpu.VMEM((TICKS, ib * SUB, bs // SUB, no * bs), jnp.float32),
                 pltpu.VMEM((NEAR, ib * SUB, bs // SUB, no * bs), jnp.int16),
                 pltpu.VMEM((NEAR, ib * SUB, 1, no * bs), jnp.float32),
-                pltpu.VMEM((TICKS + 1, ib * SUB, bs // SUB, no * bs), jnp.int16),
-                pltpu.VMEM((TICKS + 1, ib * SUB, 1, no * bs), jnp.float32),
+                pltpu.VMEM((TICKS + 3, ib * SUB, bs // SUB, no * bs), jnp.int16),
+                pltpu.VMEM((TICKS + 3, ib * SUB, 1, no * bs), jnp.float32),
                 pltpu.SMEM((TICKS + 1, ib, nl), jnp.int32),
                 pltpu.SMEM((2 * LINE, ib, no), jnp.int32),
                 dma((2,)),
-                dma((4,)), dma((4,)),
+                dma((5,)), dma((5,)),
                 dma((ib + 1,)), dma((ib + 1,)),
                 dma((3, ib + 1)), dma((3, ib + 1)),
                 dma((4, ib + 1)), dma((4, ib + 1)),
-                dma((NEAR, ib * SUB)), dma((TICKS + 1, ib * SUB)),
-                dma((NEAR, ib * SUB)), dma((TICKS + 1, ib * SUB)),
+                dma((NEAR, ib * SUB)), dma((TICKS + 3, ib * SUB)),
+                dma((NEAR, ib * SUB)), dma((TICKS + 3, ib * SUB)),
                 pltpu.SemaphoreType.REGULAR,
             ],
             compiler_params=pltpu.CompilerParams(collective_id=0, has_side_effects=True),

time: 70 us -> 68.5 us (0.979)
  the two profiles are of different devices: /device:TPU:288 before, /device:TPU:352 now
where the time goes in v4:
time: 68.5 us; the launch traced here: 68.3 us
  Pallas kernels  66.4 us (97%)
  local copies, waits for them, and re-layouts  1.89 us (3%)
    pallas_call x1, Pallas kernels, on_device(): pl.pallas_call(functools.partial(kernel, n_row, n_col), out_shape=jax.Sha...  66.4 us
    unnamed x1, local copies, waits for them, and re-layouts  1.89 us

profile of v4, /device:TPU:352, one launch (start us, length us, event | category | flops | bytes accessed | tf_op | source)
XLA Modules:
  0.0 68.3 jit_solution(3174913074130343345)
XLA Ops:
  0.0 66.4 %shard_map.55 = f32[2,8,64,64]{3,2,1,0:T(8,128)} custom-call(bf16[2,8,64,64]{3,2,1,0:T(8,128)(2,1)} %bitcast.8, s32[2,8]{1,0:T(2,128)} %bitcast.10, bf16[16,6,64,64]{3,2,1,0:T(8,128)(2,1)} %bitcast.7, s32[1,6,1,16]{3,2,1,0:T(1,128)} %bitcast.9, s32[2,8]{1,0:T(2,128)} %bitcast.11), custom_call_target="tpu_custom_call" | custom-call | tf_op jit(solution)/shard_map/pallas_call | solution.py:387
  66.4 1.9 %copy.7 = f32[1,1,2,8,64,64]{5,4,3,2,1,0:T(8,128)} copy(f32[1,1,2,8,64,64]{5,4,3,2,1,0:T(8,128)} %bitcast.6) | data formatting | bytes 524288

commit v5 on v4

--- a/solution.py
+++ b/solution.py
@@ -12,7 +12,7 @@
 LINE = 8
 QUAD = 4
 FULL = 32767.0
-SUB = 2
+SUB = 1
 MESH = pl.DeviceIdType.MESH
 
 
@@ -320,22 +320,22 @@
             down(0, g)
 
     from_far(0)
+    from_far(1)
     collect(0)
-    from_far(1)
+    collect(1)
     from_sibling(0)
+    from_sibling(1)
     products(0, 0)
+    products(0, 1)
     step(jnp.int32(0), 0)
+    step(jnp.int32(0), 1)
     products(1, 0)
+    products(1, 1)
     step(jnp.int32(1), 0)
-    collect(1)
+    step(jnp.int32(1), 1)
     products(2, 0)
+    products(2, 1)
     products(3, 0)
-    from_sibling(1)
-    products(0, 1)
-    step(jnp.int32(0), 1)
-    products(1, 1)
-    step(jnp.int32(1), 1)
-    products(2, 1)
     products(3, 1)
 
     def steps(t, carry):

time: 68.5 us -> 66.7 us (0.974)
  Pallas kernels: 66.4 us -> 64.6 us
    pallas_call x1, Pallas kernels: 66.4 us -> 64.6 us  [on_device(): pl.pallas_call(functools.partial(kernel, n_row, n_col), out_shape=jax.Sha...]
where the time goes in v5:
time: 66.7 us; the launch traced here: 66.5 us
  Pallas kernels  64.6 us (97%)
  local copies, waits for them, and re-layouts  1.89 us (3%)
    pallas_call x1, Pallas kernels, on_device(): pl.pallas_call(functools.partial(kernel, n_row, n_col), out_shape=jax.Sha...  64.6 us
    unnamed x1, local copies, waits for them, and re-layouts  1.89 us

profile of v5, /device:TPU:352, one launch (start us, length us, event | category | flops | bytes accessed | tf_op | source)
XLA Modules:
  0.0 66.5 jit_solution(595336574424461111)
XLA Ops:
  0.0 64.6 %shard_map.55 = f32[2,8,64,64]{3,2,1,0:T(8,128)} custom-call(bf16[2,8,64,64]{3,2,1,0:T(8,128)(2,1)} %bitcast.8, s32[2,8]{1,0:T(2,128)} %bitcast.10, bf16[16,6,64,64]{3,2,1,0:T(8,128)(2,1)} %bitcast.7, s32[1,6,1,16]{3,2,1,0:T(1,128)} %bitcast.9, s32[2,8]{1,0:T(2,128)} %bitcast.11), custom_call_target="tpu_custom_call" | custom-call | tf_op jit(solution)/shard_map/pallas_call | solution.py:387
  64.6 1.9 %copy.7 = f32[1,1,2,8,64,64]{5,4,3,2,1,0:T(8,128)} copy(f32[1,1,2,8,64,64]{5,4,3,2,1,0:T(8,128)} %bitcast.6) | data formatting | bytes 524288

commit v6 on v5

--- a/solution.py
+++ b/solution.py
@@ -17,8 +17,8 @@
 
 
 def kernel(
-    n_row, n_col, left_hbm, left_cols, right_hbm, right_cols, out_cols, out_ref,
-    lraw, rraw, lbuf, dense, wide, part, sent, sent_scale, got, got_scale, lcol, ocol,
+    n_row, n_col, left_hbm, left_cols, right_hbm, right_cols_hbm, out_cols, out_ref,
+    lraw, rraw, lbuf, dense, wide, part, sent, sent_scale, got, got_scale, lcol, ocol, right_cols,
     local_sem, oc_send, oc_recv, far_send, far_recv, y_send, y_recv, sib_send, sib_recv,
     sum_send, sum_recv, scale_send, scale_recv, far_ready,
 ):
@@ -33,6 +33,7 @@
     place = lax.rem(z, QUAD)
     far = lax.rem(row + 8, n_row)
     sibling = row + 1 - 2 * core
+    crosses = (y > 0) | (core > 0)
     ib, nl, bs, _ = lraw.shape
     kb = rraw.shape[0]
     nr = rraw.shape[1] - 1
@@ -41,7 +42,14 @@
 
     get_left = pltpu.make_async_copy(left_hbm, lraw, local_sem.at[0])
     get_right = pltpu.make_async_copy(right_hbm, rraw.at[:, pl.ds(0, nr)], local_sem.at[1])
+    tables = (
+        pltpu.make_async_copy(left_cols, lcol.at[0], local_sem.at[2]),
+        pltpu.make_async_copy(out_cols, ocol.at[z], local_sem.at[3]),
+        pltpu.make_async_copy(right_cols_hbm, right_cols, local_sem.at[4]),
+    )
     get_left.start()
+    for table in tables:
+        table.start()
     get_right.start()
 
     barrier = pltpu.get_barrier_semaphore()
@@ -89,11 +97,8 @@
     for b in range(ib):
         for a in range(0, nl, 2):
             lbuf[0, b, :, a * bs : (a + 2) * bs] = jnp.concatenate([lraw[b, a], lraw[b, a + 1]], axis=1)
-    for b in range(ib):
-        for a in range(nl):
-            lcol[0, b, a] = left_cols[b, a]
-        for o in range(no):
-            ocol[z, b, o] = out_cols[b, o]
+    for table in tables:
+        table.wait()
     for i in range(kb):
         rraw[i, nr] = jnp.zeros((bs, bs), rraw.dtype)
 
@@ -128,12 +133,12 @@
 
     def to_mate(i):
         return remote(
-            out_cols, ocol.at[z], oc_send.at[i - 1], oc_recv.at[i - 1], {"col": line + QUAD * upper + lax.rem(place + i, QUAD)}
+            ocol.at[z], ocol.at[z], oc_send.at[i - 1], oc_recv.at[i - 1], {"col": line + QUAD * upper + lax.rem(place + i, QUAD)}
         )
 
     def from_mate(i):
         return remote(
-            out_cols, ocol.at[QUAD * upper + lax.rem(place + QUAD - i, QUAD)], oc_send.at[i - 1], oc_recv.at[i - 1],
+            ocol.at[z], ocol.at[QUAD * upper + lax.rem(place + QUAD - i, QUAD)], oc_send.at[i - 1], oc_recv.at[i - 1],
             {"col": line + QUAD * upper + lax.rem(place + QUAD - i, QUAD)},
         )
 
@@ -149,7 +154,10 @@
     @pl.when(half == 1)
     def _():
         pl.semaphore_signal(far_ready, inc=1, device_id={"row": far}, device_id_type=MESH)
-        start(to_far(0))
+
+        @pl.when(crosses)
+        def _():
+            start(to_far(0))
 
     for i in range(1, QUAD):
         to_mate(i).start()
@@ -183,7 +191,7 @@
 
     lax.fori_loop(0, kb // 2, fill, 0)
 
-    @pl.when(half == 1)
+    @pl.when((half == 1) & crosses)
     def _():
         start(to_far(1))
 
@@ -196,8 +204,11 @@
     @pl.when(half == 0)
     def _():
         pl.semaphore_wait(far_ready, 1)
-        for b in range(ib):
-            start(to_far(b))
+
+        @pl.when(crosses)
+        def _():
+            for b in range(ib):
+                start(to_far(b))
 
     low = lax.broadcasted_iota(jnp.int32, (bs, 2 * bs), 1) < bs
 
@@ -285,7 +296,10 @@
             product(NEAR, b, 0)
 
     def from_far(b):
-        wait_recv(to_far(b))
+        @pl.when(crosses)
+        def _():
+            wait_recv(to_far(b))
+
         for d in range(1, 4):
             @pl.when(y + d >= 4)
             def _():
@@ -360,7 +374,10 @@
             out_ref[g // SUB, o, g % SUB * sub : (g % SUB + 1) * sub] = part[NEAR, g, :, o * bs : (o + 1) * bs]
 
     for b in range(ib):
-        wait_send(to_far(b))
+        @pl.when(crosses)
+        def _():
+            wait_send(to_far(b))
+
         for d in range(1, 4):
             wait_send(to_y(d, 0, b))
         for i in range(4):
@@ -387,13 +404,7 @@
         product = pl.pallas_call(
             functools.partial(kernel, n_row, n_col),
             out_shape=jax.ShapeDtypeStruct((ib, no, bs, bs), jnp.float32),
-            in_specs=[
-                pl.BlockSpec(memory_space=pl.ANY),
-                pl.BlockSpec(memory_space=pltpu.SMEM),
-                pl.BlockSpec(memory_space=pl.ANY),
-                pl.BlockSpec(memory_space=pltpu.SMEM),
-                pl.BlockSpec(memory_space=pltpu.SMEM),
-            ],
+            in_specs=[pl.BlockSpec(memory_space=pltpu.HBM)] * 5,
             out_specs=pl.BlockSpec(memory_space=pltpu.VMEM),
             scratch_shapes=[
                 pltpu.VMEM(left.shape, left.dtype),
@@ -408,7 +419,8 @@
                 pltpu.VMEM((TICKS + 3, ib * SUB, 1, no * bs), jnp.float32),
                 pltpu.SMEM((TICKS + 1, ib, nl), jnp.int32),
                 pltpu.SMEM((2 * LINE, ib, no), jnp.int32),
-                dma((2,)),
+                pltpu.SMEM(right_cols.shape, jnp.int32),
+                dma((5,)),
                 dma((5,)), dma((5,)),
                 dma((ib + 1,)), dma((ib + 1,)),
                 dma((3, ib + 1)), dma((3, ib + 1)),

time: 66.7 us -> 65.9 us (0.988)
  Pallas kernels: 64.6 us -> 63.8 us
    pallas_call x1, Pallas kernels: 64.6 us -> 63.8 us  [on_device(): pl.pallas_call(functools.partial(kernel, n_row, n_col), out_shape=jax.Sha...]
where the time goes in v6:
time: 65.9 us; the launch traced here: 65.7 us
  Pallas kernels  63.8 us (97%)
  local copies, waits for them, and re-layouts  1.89 us (3%)
    pallas_call x1, Pallas kernels, on_device(): pl.pallas_call(functools.partial(kernel, n_row, n_col), out_shape=jax.Sha...  63.8 us
    unnamed x1, local copies, waits for them, and re-layouts  1.89 us

profile of v6, /device:TPU:352, one launch (start us, length us, event | category | flops | bytes accessed | tf_op | source)
XLA Modules:
  0.0 65.7 jit_solution(11473425357226521501)
XLA Ops:
  0.0 63.8 %shard_map.55 = f32[2,8,64,64]{3,2,1,0:T(8,128)} custom-call(bf16[2,8,64,64]{3,2,1,0:T(8,128)(2,1)} %bitcast.8, s32[2,8]{1,0:T(2,128)} %bitcast.10, bf16[16,6,64,64]{3,2,1,0:T(8,128)(2,1)} %bitcast.7, s32[1,6,1,16]{3,2,1,0:T(1,128)} %bitcast.9, s32[2,8]{1,0:T(2,128)} %bitcast.11), custom_call_target="tpu_custom_call" | custom-call | tf_op jit(solution)/shard_map/pallas_call | solution.py:404
  63.8 1.9 %copy.7 = f32[1,1,2,8,64,64]{5,4,3,2,1,0:T(8,128)} copy(f32[1,1,2,8,64,64]{5,4,3,2,1,0:T(8,128)} %bitcast.6) | data formatting | bytes 524288

commit v7 on v6

--- a/solution.py
+++ b/solution.py
@@ -278,15 +278,15 @@
         s_up = t + QUAD * upper
         s_down = 2 + QUAD * upper - t
 
+        @pl.when((s_down >= 0) & (s_down < z) & ((s_down > 0) | (place < QUAD - 1)))
+        def _():
+            for g in chunks:
+                down(s_down, g)
+
         @pl.when((t >= place) & (s_up < NEAR) & (s_up > 0))
         def _():
             for g in chunks:
                 up(s_up, g)
-
-        @pl.when((s_down >= 0) & (s_down < z) & ((s_down > 0) | (place < QUAD - 1)))
-        def _():
-            for g in chunks:
-                down(s_down, g)
 
     def products(i, b):
         if i < 3:

time: 65.9 us -> 65.4 us (level)
  the two profiles are of different devices: /device:TPU:352 before, /device:TPU:384 now
where the time goes in v7:
time: 65.4 us; the launch traced here: 65.3 us
  Pallas kernels  63.4 us (97%)
  local copies, waits for them, and re-layouts  1.89 us (3%)
    pallas_call x1, Pallas kernels, on_device(): pl.pallas_call(functools.partial(kernel, n_row, n_col), out_shape=jax.Sha...  63.4 us
    unnamed x1, local copies, waits for them, and re-layouts  1.89 us

profile of v7, /device:TPU:384, one launch (start us, length us, event | category | flops | bytes accessed | tf_op | source)
XLA Modules:
  0.0 65.3 jit_solution(10849890622057896657)
XLA Ops:
  0.0 63.4 %shard_map.55 = f32[2,8,64,64]{3,2,1,0:T(8,128)} custom-call(bf16[2,8,64,64]{3,2,1,0:T(8,128)(2,1)} %bitcast.8, s32[2,8]{1,0:T(2,128)} %bitcast.10, bf16[16,6,64,64]{3,2,1,0:T(8,128)(2,1)} %bitcast.7, s32[1,6,1,16]{3,2,1,0:T(1,128)} %bitcast.9, s32[2,8]{1,0:T(2,128)} %bitcast.11), custom_call_target="tpu_custom_call" | custom-call | tf_op jit(solution)/shard_map/pallas_call | solution.py:404
  63.4 1.9 %copy.7 = f32[1,1,2,8,64,64]{5,4,3,2,1,0:T(8,128)} copy(f32[1,1,2,8,64,64]{5,4,3,2,1,0:T(8,128)} %bitcast.6) | data formatting | bytes 524288

commit v8 on v7

--- a/solution.py
+++ b/solution.py
@@ -78,15 +78,7 @@
     def _():
         greet({"col": lax.rem(col + n_col - LINE + 1, n_col)})
 
-    @pl.when(upper == 1)
-    def _():
-        greet({"col": line + QUAD - 1})
-
-    @pl.when(upper == 0)
-    def _():
-        greet({"col": lax.rem(col + n_col - QUAD - z, n_col)})
-
-    n_greeted = 9 + half + jnp.where(z == 0, 0, jnp.where(z == QUAD - 1, 5, jnp.where(z == QUAD, 4, 1)))
+    n_greeted = 9 + half + jnp.where((z == 0) | (z == QUAD), 0, 1)
 
     def remote(src, dst, send, recv, to):
         return pltpu.make_async_remote_copy(
@@ -340,8 +332,8 @@
     from_sibling(0)
     from_sibling(1)
     products(0, 0)
+    step(jnp.int32(0), 0)
     products(0, 1)
-    step(jnp.int32(0), 0)
     step(jnp.int32(0), 1)
     products(1, 0)
     products(1, 1)

time: 65.4 us -> 65 us (level)
  no operation moved by 1% of the time
where the time goes in v8:
time: 65 us; the launch traced here: 64.9 us
  Pallas kernels  63 us (97%)
  local copies, waits for them, and re-layouts  1.89 us (3%)
    pallas_call x1, Pallas kernels, on_device(): pl.pallas_call(functools.partial(kernel, n_row, n_col), out_shape=jax.Sha...  63 us
    unnamed x1, local copies, waits for them, and re-layouts  1.89 us

profile of v8, /device:TPU:384, one launch (start us, length us, event | category | flops | bytes accessed | tf_op | source)
XLA Modules:
  0.0 64.9 jit_solution(7037381681253550096)
XLA Ops:
  0.0 63.0 %shard_map.55 = f32[2,8,64,64]{3,2,1,0:T(8,128)} custom-call(bf16[2,8,64,64]{3,2,1,0:T(8,128)(2,1)} %bitcast.8, s32[2,8]{1,0:T(2,128)} %bitcast.10, bf16[16,6,64,64]{3,2,1,0:T(8,128)(2,1)} %bitcast.7, s32[1,6,1,16]{3,2,1,0:T(1,128)} %bitcast.9, s32[2,8]{1,0:T(2,128)} %bitcast.11), custom_call_target="tpu_custom_call" | custom-call | tf_op jit(solution)/shard_map/pallas_call | solution.py:396
  63.0 1.9 %copy.7 = f32[1,1,2,8,64,64]{5,4,3,2,1,0:T(8,128)} copy(f32[1,1,2,8,64,64]{5,4,3,2,1,0:T(8,128)} %bitcast.6) | data formatting | bytes 524288
